TPU v7x, 128 devices: a whole 4x4x4 slice. The times are simulated.
128 devices in a mesh: lat: 16 (over x_lo, z, core), lon: 8 (over y, x_hi).
Axes of the slice: x: 4 (x_hi: 2, x_lo: 2; x = x_hi * 2 + x_lo), y: 4, z: 4, core: 2. Of those that a mesh axis runs over, the one named last changes fastest.
Arguments:
- forcing: float32 [16, 2048, 2048], P(None, 'lat', 'lon'), may hold values from -6 to 6
- metric_lon: float32 [2048, 2048], P('lat', 'lon'), may hold values from -0.5 to 0.5
- metric_lat: float32 [2048, 2048], P('lat', 'lon'), may hold values from -0.5 to 0.5
- lon_weights: float32 [2048], P('lon'), may hold values from 0.5 to 2
- eigen_basis: float32 [2048, 2048], replicated, may hold values from -0.125 to 0.125
- lower_mult: float32 [16, 2048, 2048], P('lon', 'lat'), may hold values from -1 to 0
- pivot_inverse: float32 [16, 2048, 2048], P('lon', 'lat'), may hold values from 0 to 2
- upper_coef: float32 [16, 2048, 2048], P('lon', 'lat'), may hold values from -33554432 to 0
Outputs:
- solution: float32 [16, 2048, 2048], P(None, 'lat', 'lon')
All inputs are finite; a program needn't handle non-finite values.
Results may differ from a plain program's by a relative error of at most 0.000082.
Values sent between devices are 32-bit elements; how exact they have to be, the bound alone decides.
A program may use at most 128 MiB of HBM per device.

v0:
```python
import jax
import jax.numpy as jnp
from jax import lax
from jax.sharding import PartitionSpec as P


def padded(shard, sides, width, wrap):
    for axis, dim in sides:
        count, length = (lax.axis_size(axis), shard.shape[dim])
        up = [(i, (i + 1) % count) for i in range(count if wrap else count - 1)]
        down = [(j, i) for i, j in up]
        last = lax.slice_in_dim(shard, length - width, length, axis=dim)
        initial = lax.slice_in_dim(shard, 0, width, axis=dim)
        before = lax.ppermute(last, axis, up)
        after = lax.ppermute(initial, axis, down)
        shard = jnp.concatenate([before, shard, after], axis=dim)
    return shard


def copy_for_each(shard, axis):
    count = lax.axis_size(axis)
    return lax.all_to_all(
        jnp.broadcast_to(shard[None], (count, *shard.shape)), axis, 0, 0, tiled=True
    )


def gathered_once(shard, axis):
    leaves = jax.tree.leaves(shard)
    sequence = sorted(range(len(leaves)), key=lambda k: -leaves[k].size)
    width = (1, *leaves[sequence[0]].shape)[-1]
    lines = [
        jnp.pad(leaves[k].reshape(-1), (0, -leaves[k].size % width)).reshape(-1, width)
        for k in sequence
    ]
    both, at, found = (copy_for_each(jnp.concatenate(lines), axis), 0, {})
    for k, line in zip(sequence, lines):
        slab = both[:, at : at + len(line)].reshape(len(both), -1)
        found[k] = slab[:, : leaves[k].size].reshape(-1, *leaves[k].shape)
        at += len(line)
    numbers = iter(range(len(leaves)))
    return jax.tree.map(lambda _: found[next(numbers)], shard)


def folded_in_pairs(pieces, combine):
    while len(jax.tree.leaves(pieces)[0]) > 1:
        pieces = jax.vmap(combine)(
            *(jax.tree.map(lambda part: part[side::2], pieces) for side in (0, 1))
        )
    return jax.tree.map(lambda part: part[0], pieces)


def carried_in(shard, axis, combine, identity):
    count, position = (lax.axis_size(axis), lax.axis_index(axis))
    passed = jnp.arange(count) < position

    def carried_kept(part, zero, own):
        part = jnp.where(
            passed.reshape(-1, *(1 for _ in own.shape)), part, jnp.asarray(zero, own.dtype)
        )
        return part

    pieces = gathered_once(shard, axis)
    return folded_in_pairs(jax.tree.map(carried_kept, pieces, identity, shard), combine)


def collected_alike(shard, axis):
    leaves, found = (jax.tree.leaves(shard), {})
    for initial, a in enumerate(leaves):
        if initial not in found:
            alike = [k for k, b in enumerate(leaves) if b.dtype == a.dtype]
            got = (
                gathered_once([leaves[k] for k in alike], axis)
                if len(alike) > 1
                else [copy_for_each(a, axis)]
            )
            for k, b in zip(alike, got):
                found[k] = b
    numbers = iter(range(len(leaves)))
    return jax.tree.map(lambda _: found[next(numbers)], shard)


def entering_2(shard, axis, combine, identity):
    count, position = (lax.axis_size(axis), lax.axis_index(axis))
    passed = jnp.arange(count) > position

    def entering_kept(part, zero, own):
        part = jnp.where(
            passed.reshape(-1, *(1 for _ in own.shape)), part, jnp.asarray(zero, own.dtype)
        )
        return part[::-1]

    pieces = collected_alike(shard, axis)
    return folded_in_pairs(jax.tree.map(entering_kept, pieces, identity, shard), combine)


def compose(earlier, later):
    return (later[0] * earlier[0], later[0] * earlier[1] + later[1])


def band_recurrence(factor, source, reverse_order):
    modes, rows, columns = factor.shape
    block = min(8, rows)
    groups = rows // block
    factor_blocks = factor.reshape(modes, groups, block, columns)
    source_blocks = source.reshape(modes, groups, block, columns)
    order = list(range(block))
    if reverse_order:
        order = order[::-1]
    running_scale = jnp.ones((modes, groups, columns), jnp.float32)
    running_shift = jnp.zeros((modes, groups, columns), jnp.float32)
    scale_rows = [None] * block
    shift_rows = [None] * block
    for position in order:
        step_factor = factor_blocks[:, :, position, :]
        running_scale = step_factor * running_scale
        running_shift = step_factor * running_shift + source_blocks[:, :, position, :]
        scale_rows[position] = running_scale
        shift_rows[position] = running_shift
    group_order = list(range(groups))
    if reverse_order:
        group_order = group_order[::-1]
    carry_scale = jnp.ones((modes, columns), jnp.float32)
    carry_shift = jnp.zeros((modes, columns), jnp.float32)
    enter_scale = [None] * groups
    enter_shift = [None] * groups
    for group in group_order:
        enter_scale[group] = carry_scale
        enter_shift[group] = carry_shift
        carry_scale, carry_shift = compose(
            (carry_scale, carry_shift), (running_scale[:, group, :], running_shift[:, group, :])
        )
    local_scale = jnp.stack(scale_rows, axis=2)
    local_shift = jnp.stack(shift_rows, axis=2)
    group_scale = jnp.stack(enter_scale, axis=1)[:, :, None, :]
    group_shift = jnp.stack(enter_shift, axis=1)[:, :, None, :]
    full_scale = (local_scale * group_scale).reshape(modes, rows, columns)
    full_shift = (local_shift + local_scale * group_shift).reshape(modes, rows, columns)
    return (full_scale, full_shift, (carry_scale, carry_shift))


def per_device(
    forcing, metric_lon, metric_lat, lon_weights, eigen_basis, lower_mult, pivot_inverse, upper_coef
):
    wrapped = padded(forcing, (("lon", 2),), 1, True)
    stacked = padded(forcing, (("lat", 1),), 1, False)
    source_term = (
        forcing
        + metric_lon * (wrapped[:, :, :-2] + wrapped[:, :, 2:])
        + metric_lat * (stacked[:, :-2, :] + stacked[:, 2:, :])
    )
    weighted = source_term * lon_weights
    spectral = jnp.einsum(
        "kji,im->kjm",
        lax.all_to_all(weighted, "lon", split_axis=0, concat_axis=2, tiled=True),
        eigen_basis,
        precision=lax.Precision.HIGHEST,
    )
    down_scale, down_shift, down_summary = band_recurrence(-lower_mult, spectral, False)
    identity = (jnp.ones_like(down_summary[0]), jnp.zeros_like(down_summary[1]))
    entering = carried_in(down_summary, "lat", compose, identity)[1]
    sweep = down_shift + down_scale * entering[:, None, :]
    up_factor = -(upper_coef * pivot_inverse)
    up_source = pivot_inverse * sweep
    up_scale, up_shift, up_summary = band_recurrence(up_factor, up_source, True)
    identity_up = (jnp.ones_like(up_summary[0]), jnp.zeros_like(up_summary[1]))
    arriving = entering_2(up_summary, "lat", compose, identity_up)[1]
    modal = up_shift + up_scale * arriving[:, None, :]
    on_grid = jnp.einsum("kjm,im->kji", modal, eigen_basis, precision=lax.Precision.HIGHEST)
    return lax.all_to_all(on_grid, "lon", split_axis=2, concat_axis=0, tiled=True)


def solution(mesh):
    placed = (
        P(None, "lat", "lon"),
        P("lat", "lon"),
        P("lat", "lon"),
        P("lon"),
        P(),
        P("lon", "lat", None),
        P("lon", "lat", None),
        P("lon", "lat", None),
    )
    return jax.shard_map(
        per_device, mesh=mesh, in_specs=placed, out_specs=P(None, "lat", "lon"), check_vma=False
    )
```

profile of v0, /device:TPU:1, one launch (start us, length us, event | category | flops | bytes accessed | tf_op | source)
XLA Modules:
  0.0 222.3 jit_solution(854617699514591773)
XLA Ops:
  1.0 4.9 %collective-permute-start.2 = (f32[16,1,256]{2,1,0:T(1,128)S(1)}, f32[16,1,256]{2,1,0:T(1,128)S(1)}, u32[]{:S(2)}, u32[]{:S(2)}) collective-permute-start(f32[16,1,256]{2,1,0:T(1,128)S(1)} %get-tuple-element.92), channel_id=1, source_target_pairs={{0,8},{8,16},{16,24},{24,32},{32,40},{40,48},{48,56},{56,64},{64,7... | collective-permute-start | bytes 49160 | tf_op jit(solution)/shard_map/ppermute | solution.py:14
  5.9 1.9 collective-permute-start.3
  7.9 2.9 %fusion.108 = (f32[16,128,1]{2,1,0:T(8,128)}, f32[16,128,1]{2,1,0:T(8,128)S(1)}) fusion(f32[16,128,256]{2,1,0:T(8,128)} %param.8), kind=kLoop, calls=%fused_computation.380 | loop fusion | bytes 32768 | tf_op jit(solution)/shard_map/slice | solution.py:12
  10.7 1.7 copy.151
  12.5 2.8 %collective-permute-start = (f32[16,128,1]{1,0,2:T(8,128)S(1)}, f32[16,128,1]{1,0,2:T(8,128)S(1)}, u32[]{:S(2)}, u32[]{:S(2)}) collective-permute-start(f32[16,128,1]{1,0,2:T(8,128)S(1)} %copy.151), channel_id=1, source_target_pairs={{0,1},{1,2},{2,3},{3,4},{4,5},{5,6},{6,7},{7,0},{8,9},{9,10},{10,1... | collective-permute-start | bytes 24584 | tf_op jit(solution)/shard_map/ppermute | solution.py:14
  15.6 2.5 %collective-permute-start.1 = (f32[16,128,1]{1,0,2:T(8,128)S(1)}, f32[16,128,1]{1,0,2:T(8,128)S(1)}, u32[]{:S(2)}, u32[]{:S(2)}) collective-permute-start(f32[16,128,1]{1,0,2:T(8,128)S(1)} %copy.152), channel_id=1, source_target_pairs={{1,0},{2,1},{3,2},{4,3},{5,4},{6,5},{7,6},{0,7},{9,8},{10,9},{11,1... | collective-permute-start | bytes 24584 | tf_op jit(solution)/shard_map/ppermute | solution.py:15
  21.0 4.0 %fusion.7 = f32[16,128,256]{2,1,0:T(8,128)} fusion(f32[16,1,256]{2,1,0:T(1,128)S(1)} %collective-permute-done.3, f32[16,128,256]{2,1,0:T(8,128)S(1)} %copy-done.1, f32[16,1,256]{2,1,0:T(1,128)S(1)} %collective-permute-done.2, f32[16,128,1]{2,1,0:T(8,128)} %copy.101, f32[16,128,1]{2,1,0:T(8,128)S(1)} %copy.99, f32[256]{0:T(256)S(1)} %copy-done.22, ...), kind=kLoop, calls=%fused_computation.8 | loop fusion | flops 5767168 | bytes 4506624 | tf_op jit(solution)/shard_map/mul | solution.py:151
  25.0 6.1 %all-to-all-start = ((f32[16,128,256]{2,1,0:T(8,128)}), f32[16,128,256]{2,1,0:T(8,128)S(1)}, u32[]{:S(2)}, u32[]{:S(2)}) async-start(f32[16,128,256]{2,1,0:T(8,128)} %fusion.7), calls=%async_computation | async-start | bytes 4194304 | tf_op jit(solution)/shard_map/all_to_all | solution.py:154
  32.3 3.1 %negate_bitcast_fusion = f32[2,16,8,2048]{3,2,1,0:T(8,128)} fusion(f32[2,128,2048]{2,1,0:T(8,128)} %param.13), kind=kLoop, calls=%fused_computation.27 | loop fusion | flops 524288 | bytes 4194304 | tf_op jit(solution)/shard_map/reshape | solution.py:104
  35.4 24.1 %all-to-all-done = f32[16,128,256]{2,1,0:T(8,128)S(1)} async-done(((f32[16,128,256]{2,1,0:T(8,128)}), f32[16,128,256]{2,1,0:T(8,128)S(1)}, u32[]{:S(2)}, u32[]{:S(2)}) %all-to-all-start) | async-done | bytes 2097184 | tf_op jit(solution)/shard_map/all_to_all | solution.py:154
  59.5 2.5 %copy.532 = f32[8,2,128,256]{3,0,2,1:T(8,128)} copy(f32[8,2,128,256]{3,2,1,0:T(8,128)S(1)} %bitcast.627) | data formatting | bytes 4194304 | tf_op jit(solution)/shard_map/all_to_all | solution.py:154
  62.0 1.7 dot_general.8
  63.8 17.1 %fusion = f32[2,16,8,2048]{3,2,1,0:T(8,128)S(1)} fusion(f32[2,16,8,2048]{3,2,1,0:T(8,128)S(1)} %dot_general.8, f32[2048,2048]{1,0:T(8,128)} %param.12), kind=kOutput, calls=%fused_computation | convolution fusion | flops 12884901888 | bytes 20971520 | tf_op jit(solution)/shard_map/kji,im->kjm/dot_general | solution.py:152
  80.9 3.2 %fusion.107 = (f32[2,16,1,2048]{3,2,1,0:T(1,128)S(1)}, f32[2,16,1,2048]{3,2,1,0:T(1,128)S(1)}, f32[2,16,1,2048]{3,2,1,0:T(1,128)S(1)}, f32[2,16,1,2048]{3,2,1,0:...) fusion(f32[2,16,8,2048]{3,2,1,0:T(8,128)S(1)} %fusion, ...), kind=kLoop, calls=%fused_computation.379 | loop fusion | bytes 8388608 | tf_op jit(solution)/shard_map/slice | solution.py:116
  85.4 2.2 fusion.33
  90.8 7.0 %all-to-all-start.1 = ((f32[16,4,2048]{2,1,0:T(4,128)}), f32[16,4,2048]{2,1,0:T(4,128)}, u32[]{:S(2)}, u32[]{:S(2)}) async-start(f32[16,4,2048]{2,1,0:T(4,128)} %broadcast_in_dim.48), calls=%async_computation.1 | async-start | bytes 1048576 | tf_op jit(solution)/shard_map/all_to_all | solution.py:22
  101.0 1.9 constant_dynamic-update-slice_fusion.3
  104.2 1.7 constant_dynamic-update-slice_fusion.1
  108.9 4.1 %multiply_add_fusion.1 = (f32[8,4,8,2048]{3,0,1,2:T(8,128)S(1)}, f32[8,4,8,2048]{3,0,1,2:T(8,128)}) fusion(f32[8,4,8,2048]{3,0,1,2:T(8,128)} %bitcast.632, f32[8,4,8,2048]{3,0,1,2:T(8,128)} %bitcast.633, f32[8,4,2048]{2,0,1:T(8,128)S(1)} %bitcast.635, f32[8,4,2048]{2,0,1:T(8,128)S(1)} %bitcast.634), kind=kLoop, calls=%fused_computation.26 | loop fusion | flops 1572864 | bytes 8912896 | tf_op jit(solution)/shard_map/add | solution.py:137
  113.1 1.7 slice_select_fusion.3
  115.1 4.9 %fusion.16 = (f32[2,16,8,2048]{3,2,1,0:T(8,128)S(1)}, f32[2,16,8,2048]{3,2,1,0:T(8,128)S(1)}) fusion(f32[2,128,2048]{2,1,0:T(8,128)} %param.14, f32[2,16,8,2048]{3,0,1,2:T(2,128)S(1)} %bitcast.626, f32[2,16,8,2048]{3,0,1,2:T(2,128)S(1)} %bitcast.625, f32[2,2048]{1,0:T(2,128)S(1)} %fusion.49, f32[2,128,2048]{2,1,0:T(8,128)} %param.15), kind=kLoop, calls=%fused_computation.21 | loop fusion | flops 2621440 | bytes 12599296 | tf_op jit(solution)/shard_map/reshape | solution.py:105
  123.0 2.4 %bitcast_add_fusion.1 = (f32[2,16,2048]{2,0,1:T(2,128)S(1)}, f32[2,16,2048]{2,0,1:T(2,128)S(1)}) fusion(f32[2,16,1,2048]{3,2,1,0:T(1,128)S(1)} %get-tuple-element.75, f32[2,16,1,2048]{3,2,1,0:T(1,128)S(1)} %get-tuple-element.69, f32[2,16,1,2048]{3,2,1,0:T(1,128)S(1)} %get-tuple-element.70, f32[2,16,1,2048]{3,2,1,0:T(1,128)S(1)} %get-tuple-element.71, ...), kind=kLoop, calls=%fused_computation.37 | loop fusion | flops 1507328 | bytes 4718592 | tf_op jit(solution)/shard_map/add | solution.py:116
  125.8 3.7 %add_dynamic-update-slice_fusion = (f32[2,16,8,2048]{3,0,1,2:T(2,128)}, f32[2,16,1,2048]{3,0,1,2:T(2,128)}, f32[2,16,1,2048]{3,0,1,2:T(2,128)S(1)}, f32[2,16,1,2...) fusion(f32[2,16,1,2048]{3,2,1,0:T(1,128)S(1)} %get-tuple-elemen, ...), kind=kLoop, calls=%fused_computation.85 | loop fusion | flops 1507326 | bytes 6029312
  132.3 5.7 %all-to-all-start.2 = ((f32[16,4,2048]{2,1,0:T(4,128)}), f32[16,4,2048]{2,1,0:T(4,128)}, u32[]{:S(2)}, u32[]{:S(2)}) async-start(f32[16,4,2048]{2,1,0:T(4,128)} %broadcast_in_dim.52), calls=%async_computation.2 | async-start | bytes 1048576 | tf_op jit(solution)/shard_map/all_to_all | solution.py:22
  138.0 2.3 %constant_dynamic-update-slice_fusion.52 = (f32[2,16,8,2048]{3,0,1,2:T(2,128)}, f32[2,16,8,2048]{3,0,1,2:T(2,128)}) fusion(f32[2,16,8,2048]{3,0,1,2:T(2,128)} %get-tuple-element.13, f32[2,16,1,2048]{3,2,1,0:T(1,128)S(1)} %get-tuple-element.69, f32[2,16,1,2048]{3,0,1,2:T(2,128)} %get-tuple-element.14, f32[2,16,1,2048]{3,2,1,0:T(1,128)S(1)} %get-tuple-element.107, ...), kind=kLoop, calls=%fused_computation.153 | loop fusion | flops 196608 | bytes 1572864
  140.3 1.7 constant_dynamic-update-slice_fusion.51
  150.0 4.2 %multiply_add_fusion = (f32[8,4,8,2048]{3,0,1,2:T(8,128)S(1)}, f32[8,4,8,2048]{3,0,1,2:T(8,128)}) fusion(f32[8,4,8,2048]{3,0,1,2:T(8,128)} %bitcast.630, f32[8,4,8,2048]{3,0,1,2:T(8,128)} %bitcast.631, f32[8,4,2048]{2,0,1:T(8,128)S(1)} %bitcast.636, f32[8,4,2048]{2,0,1:T(8,128)S(1)} %bitcast.637), kind=kLoop, calls=%fused_computation.25 | loop fusion | flops 1572864 | bytes 8912896 | tf_op jit(solution)/shard_map/add | solution.py:137
  154.2 1.7 slice_select_fusion.1
  156.2 27.4 %fusion.2 = f32[2,128,2048]{2,1,0:T(8,128)} fusion(f32[2048,2048]{1,0:T(8,128)} %param.12, f32[2,16,8,2048]{3,0,1,2:T(2,128)S(1)} %bitcast.624, f32[2,16,8,2048]{3,0,1,2:T(2,128)S(1)} %bitcast.623, f32[2,2048]{1,0:T(2,128)S(1)} %fusion.47), kind=kOutput, calls=%fused_computation.2 | convolution fusion | flops 12885950464 | bytes 23085056 | tf_op jit(solution)/shard_map/kjm,im->kji/dot_general | solution.py:168
  183.6 2.8 %copy.146 = f32[2,128,2048]{1,0,2:T(2,128)S(1)} copy(f32[2,128,2048]{2,1,0:T(8,128)} %fusion.2) | data formatting | bytes 4194304 | tf_op jit(solution)/shard_map/kjm,im->kji/dot_general | solution.py:168
  186.5 31.5 %all_to_all.43 = f32[2,128,2048]{1,0,2:T(2,128)} all-to-all(f32[2,128,2048]{1,0,2:T(2,128)S(1)} %copy.146), channel_id=1, replica_groups=mesh['lat'=16,'lon'=8] {'lon'}, dimensions={2} | all-to-all | bytes 4194304 | tf_op jit(solution)/shard_map/all_to_all | solution.py:169
  218.0 4.1 %copy.147 = f32[8,2,128,256]{3,2,1,0:T(8,128)} copy(f32[8,2,128,256]{2,1,3,0:T(2,128)} %bitcast.629) | data formatting | bytes 4194304 | tf_op jit(solution)/shard_map/all_to_all | solution.py:169
  (152 shorter events, 31.8 us)
Async XLA Ops:
  1.0 20.0 %collective-permute-start.2 = (f32[16,1,256]{2,1,0:T(1,128)S(1)}, f32[16,1,256]{2,1,0:T(1,128)S(1)}, u32[]{:S(2)}, u32[]{:S(2)}) collective-permute-start(f32[16,1,256]{2,1,0:T(1,128)S(1)} %get-tuple-element.92), channel_id=1, source_target_pairs={{0,8},{8,16},{16,24},{24,32},{32,40},{40,48},{48,56},{56,64},{64,7... | collective-permute-start | bytes 49160 | tf_op jit(solution)/shard_map/ppermute | solution.py:14
  5.9 15.0 %collective-permute-start.3 = (f32[16,1,256]{2,1,0:T(1,128)S(1)}, f32[16,1,256]{2,1,0:T(1,128)S(1)}, u32[]{:S(2)}, u32[]{:S(2)}) collective-permute-start(f32[16,1,256]{2,1,0:T(1,128)S(1)} %get-tuple-element.93), channel_id=1, source_target_pairs={{8,0},{16,8},{24,16},{32,24},{40,32},{48,40},{56,48},{64,56},{72,6... | collective-permute-start | bytes 49160 | tf_op jit(solution)/shard_map/ppermute | solution.py:15
  10.7 10.2 %copy-start.1 = (f32[16,128,256]{2,1,0:T(8,128)S(1)}, f32[16,128,256]{2,1,0:T(8,128)}, u32[]{:S(2)}) copy-start(f32[16,128,256]{2,1,0:T(8,128)} %param.8) | copy-start | bytes 6291460
  10.7 10.2 %copy-start.20 = (f32[128,256]{1,0:T(8,128)S(1)}, f32[128,256]{1,0:T(8,128)}, u32[]{:S(2)}) copy-start(f32[128,256]{1,0:T(8,128)} %param.10) | copy-start | bytes 393220
  10.7 10.2 %copy-start.21 = (f32[128,256]{1,0:T(8,128)S(1)}, f32[128,256]{1,0:T(8,128)}, u32[]{:S(2)}) copy-start(f32[128,256]{1,0:T(8,128)} %param.9) | copy-start | bytes 393220
  10.7 10.3 %copy-start.22 = (f32[256]{0:T(256)S(1)}, f32[256]{0:T(256)}, u32[]{:S(2)}) copy-start(f32[256]{0:T(256)} %param.11) | copy-start | bytes 3076
  12.5 6.3 %collective-permute-start = (f32[16,128,1]{1,0,2:T(8,128)S(1)}, f32[16,128,1]{1,0,2:T(8,128)S(1)}, u32[]{:S(2)}, u32[]{:S(2)}) collective-permute-start(f32[16,128,1]{1,0,2:T(8,128)S(1)} %copy.151), channel_id=1, source_target_pairs={{0,1},{1,2},{2,3},{3,4},{4,5},{5,6},{6,7},{7,0},{8,9},{9,10},{10,1... | collective-permute-start | bytes 24584 | tf_op jit(solution)/shard_map/ppermute | solution.py:14
  15.6 4.0 %collective-permute-start.1 = (f32[16,128,1]{1,0,2:T(8,128)S(1)}, f32[16,128,1]{1,0,2:T(8,128)S(1)}, u32[]{:S(2)}, u32[]{:S(2)}) collective-permute-start(f32[16,128,1]{1,0,2:T(8,128)S(1)} %copy.152), channel_id=1, source_target_pairs={{1,0},{2,1},{3,2},{4,3},{5,4},{6,5},{7,6},{0,7},{9,8},{10,9},{11,1... | collective-permute-start | bytes 24584 | tf_op jit(solution)/shard_map/ppermute | solution.py:15
  25.0 34.5 %all-to-all-start = ((f32[16,128,256]{2,1,0:T(8,128)}), f32[16,128,256]{2,1,0:T(8,128)S(1)}, u32[]{:S(2)}, u32[]{:S(2)}) async-start(f32[16,128,256]{2,1,0:T(8,128)} %fusion.7), calls=%async_computation | async-start | bytes 4194304 | tf_op jit(solution)/shard_map/all_to_all | solution.py:154
  63.7 17.2 %copy-start.3 = (f32[2,16,8,2048]{3,2,1,0:T(8,128)S(1)}, f32[2,16,8,2048]{3,2,1,0:T(8,128)}, u32[]{:S(2)}) copy-start(f32[2,16,8,2048]{3,2,1,0:T(8,128)} %negate_bitcast_fusion) | copy-start | bytes 6291460
  84.2 3.4 %copy-start.4 = (f32[2,16,1,2048]{3,2,1,0:T(1,128)}, f32[2,16,1,2048]{3,2,1,0:T(1,128)S(1)}, u32[]{:S(2)}) copy-start(f32[2,16,1,2048]{3,2,1,0:T(1,128)S(1)} %get-tuple-element.189) | copy-start | bytes 786436
  84.2 3.4 %copy-start.6 = (f32[2,16,1,2048]{3,2,1,0:T(1,128)}, f32[2,16,1,2048]{3,2,1,0:T(1,128)S(1)}, u32[]{:S(2)}) copy-start(f32[2,16,1,2048]{3,2,1,0:T(1,128)S(1)} %get-tuple-element.85) | copy-start | bytes 786436
  84.2 3.4 %copy-start.8 = (f32[2,16,1,2048]{3,2,1,0:T(1,128)}, f32[2,16,1,2048]{3,2,1,0:T(1,128)S(1)}, u32[]{:S(2)}) copy-start(f32[2,16,1,2048]{3,2,1,0:T(1,128)S(1)} %get-tuple-element.186) | copy-start | bytes 786436
  85.4 2.8 %copy-start.13 = (f32[2,16,2048]{2,0,1:T(2,128)S(1)}, f32[2,16,2048]{2,0,1:T(2,128)}, u32[]{:S(2)}) copy-start(f32[2,16,2048]{2,0,1:T(2,128)} %constant_dynamic-update-slice_fusion.29) | copy-start | bytes 786436
  87.6 1.2 copy-start.10
  88.8 1.1 copy-start.14
  89.2 0.7 copy-start.11
  90.8 22.3 %all-to-all-start.1 = ((f32[16,4,2048]{2,1,0:T(4,128)}), f32[16,4,2048]{2,1,0:T(4,128)}, u32[]{:S(2)}, u32[]{:S(2)}) async-start(f32[16,4,2048]{2,1,0:T(4,128)} %broadcast_in_dim.48), calls=%async_computation.1 | async-start | bytes 1048576 | tf_op jit(solution)/shard_map/all_to_all | solution.py:22
  97.8 3.2 %copy-start.7 = (f32[2,16,1,2048]{3,2,1,0:T(1,128)S(1)}, f32[2,16,1,2048]{3,2,1,0:T(1,128)}, u32[]{:S(2)}) copy-start(f32[2,16,1,2048]{3,2,1,0:T(1,128)} %copy-done.6) | copy-start | bytes 786436
  97.8 3.1 %copy-start.9 = (f32[2,16,1,2048]{3,2,1,0:T(1,128)S(1)}, f32[2,16,1,2048]{3,2,1,0:T(1,128)}, u32[]{:S(2)}) copy-start(f32[2,16,1,2048]{3,2,1,0:T(1,128)} %copy-done.8) | copy-start | bytes 786436
  104.2 3.1 %copy-start.5 = (f32[2,16,1,2048]{3,2,1,0:T(1,128)S(1)}, f32[2,16,1,2048]{3,2,1,0:T(1,128)}, u32[]{:S(2)}) copy-start(f32[2,16,1,2048]{3,2,1,0:T(1,128)} %copy-done.4) | copy-start | bytes 786436
  106.0 2.9 %copy-start.12 = (f32[2,16,2048]{2,0,1:T(2,128)S(1)}, f32[2,16,2048]{2,0,1:T(2,128)}, u32[]{:S(2)}) copy-start(f32[2,16,2048]{2,0,1:T(2,128)} %copy-done.11) | copy-start | bytes 786436
  106.0 2.9 %copy-start.15 = (f32[2,16,2048]{2,0,1:T(2,128)S(1)}, f32[2,16,2048]{2,0,1:T(2,128)}, u32[]{:S(2)}) copy-start(f32[2,16,2048]{2,0,1:T(2,128)} %copy-done.14) | copy-start | bytes 786436
  113.1 2.0 copy-start.2
  130.0 0.7 copy-start.16
  130.7 0.7 copy-start.18
  132.3 21.9 %all-to-all-start.2 = ((f32[16,4,2048]{2,1,0:T(4,128)}), f32[16,4,2048]{2,1,0:T(4,128)}, u32[]{:S(2)}, u32[]{:S(2)}) async-start(f32[16,4,2048]{2,1,0:T(4,128)} %broadcast_in_dim.52), calls=%async_computation.2 | async-start | bytes 1048576 | tf_op jit(solution)/shard_map/all_to_all | solution.py:22
  145.5 4.5 %copy-start.17 = (f32[2,16,2048]{2,0,1:T(2,128)S(1)}, f32[2,16,2048]{2,0,1:T(2,128)}, u32[]{:S(2)}) copy-start(f32[2,16,2048]{2,0,1:T(2,128)} %copy-done.16) | copy-start | bytes 786436
  145.5 4.5 %copy-start.19 = (f32[2,16,2048]{2,0,1:T(2,128)S(1)}, f32[2,16,2048]{2,0,1:T(2,128)}, u32[]{:S(2)}) copy-start(f32[2,16,2048]{2,0,1:T(2,128)} %copy-done.18) | copy-start | bytes 786436
  154.2 2.1 copy-start
where the time goes:
time: 226 us; the launch traced here: 222 us
  other arithmetic  53.2 us (24%)
  matrix products  44.6 us (20%)
  local copies, waits for them, and re-layouts  36.1 us (16%)
  blocking collectives  31.5 us (14%)
  starting transfers between devices  30.9 us (14%)
  waiting for transfers between devices  25.3 us (11%)
    all_to_all x1, blocking collectives, per_device(): lax.all_to_all(on_grid, 'lon', split_axis=2, concat_axis=0, tiled=True)  31.5 us
    dot_general x1, matrix products, per_device(): jnp.einsum('kjm,im->kji', modal, eigen_basis, precision=lax.Precision.HIG...  27.4 us
    all_to_all x1, waiting for transfers between devices, per_device(): lax.all_to_all(weighted, 'lon', split_axis=0, concat_axis=2, tiled=True)  24.1 us
    unnamed x49, other arithmetic  20.7 us
    dot_general x1, matrix products, per_device(): jnp.einsum('kji,im->kjm', lax.all_to_all(weighted, 'lon', split_axis=0, c...  17.1 us
    all_to_all x2, starting transfers between devices, copy_for_each(): lax.all_to_all(jnp.broadcast_to(shard[None], (count, *shard.shape)), axis...  12.7 us
    unnamed x69, local copies, waits for them, and re-layouts  10.1 us
    add x2, other arithmetic, band_recurrence(): local_shift + local_scale * group_shift  8.31 us
  transfers between devices with their start and end apart: 7, of which 3 were waited for; matrix products, arithmetic and copies ran while one was open for 19% of the time, Pallas kernels for 0%

commit v1 on v0

v1 whole, which is shorter than its diff:
```python
import functools

import jax
import jax.numpy as jnp
from jax import lax
from jax.experimental import pallas as pl
from jax.experimental.pallas import tpu as pltpu
from jax.sharding import PartitionSpec as P

MESH = pl.DeviceIdType.MESH
F32, BF16 = jnp.float32, jnp.bfloat16
NN = (((1,), (0,)), ((), ()))
NT = (((1,), (1,)), ((), ()))
TILES = 4
STEPS = 16


def split(x):
    high = x.astype(BF16)
    return high, (x - high.astype(F32)).astype(BF16)


def product(lhs_high, lhs_low, rhs_high, rhs_low, dims):
    dot = functools.partial(lax.dot_general, dimension_numbers=dims, preferred_element_type=F32)
    return dot(lhs_high, rhs_high) + dot(lhs_high, rhs_low) + dot(lhs_low, rhs_high)


def segments_combined(scale, shift, forward):
    row = lax.broadcasted_iota(jnp.int32, scale.shape, 0)

    def moved(x, by):
        return pltpu.roll(x, by if forward else 8 - by, 0)

    def inside(by):
        return row >= by if forward else row < 8 - by

    for by in (1, 2, 4):
        keep = inside(by)
        shift = jnp.where(keep, scale * moved(shift, by) + shift, shift)
        scale = jnp.where(keep, scale * moved(scale, by), scale)
    first = inside(1)
    return (
        scale,
        shift,
        jnp.where(first, moved(scale, 1), 1.0),
        jnp.where(first, moved(shift, 1), 0.0),
    )


def kernel(
    forcing_h, mlon_h, mlat_h, wlon_h, basis_h, low_h, pinv_h, up_h, out_h,
    fpad, mlon, mlat, wlon, row_last, row_first, halo_n, halo_s, edge, halo_w, halo_e, halo_t,
    send1, got1, stage, vh, vl, low, pinv, up, pref, qref, wref,
    xh, xl, body, seg_eq, seg_ew, seg_eb, gc, gd, send2,
    l_in, l_v, l_co, l_own, h_s, h_r, s1, r1, c_s, c_r, d_s, d_r, s2, r2,
):
    a, b = lax.axis_index("lat"), lax.axis_index("lon")
    chip, core = lax.div(a, 2), lax.rem(a, 2)
    copy = pltpu.make_async_copy

    inputs = [
        copy(forcing_h, fpad.at[:, pl.ds(8, 128), :], l_in.at[0]),
        copy(mlon_h, mlon, l_in.at[1]),
        copy(mlat_h, mlat, l_in.at[2]),
        copy(wlon_h, wlon, l_in.at[3]),
    ]
    for c in inputs:
        c.start()

    def basis_rows(i, slot):
        rows = pl.multiple_of(i * 128, 128)
        return copy(basis_h.at[pl.ds(rows, 128)], stage.at[slot], l_v.at[slot])

    coefs = [
        copy(src.at[:, :, pl.ds(c * 128, 128)], dst.at[:, c], l_co.at[i, c])
        for i, (src, dst) in enumerate(((low_h, low), (pinv_h, pinv), (up_h, up)))
        for c in range(16)
    ]

    def lon_peer(o):
        return {"lon": lax.rem(b + o, 8)}

    def lat_peer(o):
        return {"lat": lax.rem(chip + o, 8) * 2 + core}

    partner = {"lat": chip * 2 + 1 - core}
    north, south = {"lat": lax.rem(a + 15, 16)}, {"lat": lax.rem(a + 1, 16)}

    barrier = pltpu.get_barrier_semaphore()
    for peer in [lon_peer(o) for o in range(1, 8)] + [lat_peer(o) for o in range(1, 8)] + [north, south]:
        pl.semaphore_signal(barrier, inc=1, device_id=peer, device_id_type=MESH)

    inputs[0].wait()
    for slot in range(4):
        basis_rows(slot, slot).start()
    for c in coefs:
        c.start()
    lane = lax.broadcasted_iota(jnp.int32, (128, 128), 1)
    columns = jnp.zeros((128, 128), F32)
    for k in range(16):
        row_first[k : k + 1, :] = fpad[k, 8:9, :]
        row_last[k : k + 1, :] = fpad[k, 135:136, :]
        columns = jnp.where(lane == k, fpad[k, 8:136, 255:256], columns)
        columns = jnp.where(lane == 16 + k, fpad[k, 8:136, 0:1], columns)
    edge[...] = columns.T[:32]
    pl.semaphore_wait(barrier, 16)

    def remote(src, dst, send, recv, peer):
        return pltpu.make_async_remote_copy(
            src_ref=src, dst_ref=dst, send_sem=send, recv_sem=recv, device_id=peer, device_id_type=MESH
        )

    halos = [
        remote(edge.at[pl.ds(0, 16)], halo_w, h_s.at[0], h_r.at[0], lon_peer(1)),
        remote(edge.at[pl.ds(16, 16)], halo_e, h_s.at[1], h_r.at[1], lon_peer(7)),
        remote(row_last, halo_n, h_s.at[2], h_r.at[2], south),
        remote(row_first, halo_s, h_s.at[3], h_r.at[3], north),
    ]
    for c in halos:
        c.start()
    for c in inputs[1:]:
        c.wait()
    for c in halos:
        c.wait()
    for k in range(16):
        fpad[k, 7:8, :] = jnp.where(a > 0, halo_n[k : k + 1, :], 0.0)
        fpad[k, 136:137, :] = jnp.where(a < 15, halo_s[k : k + 1, :], 0.0)
    halo_t[...] = jnp.concatenate([halo_w[...], halo_e[...], jnp.zeros((96, 128), F32)], axis=0).T

    lane2 = lax.broadcasted_iota(jnp.int32, (32, 256), 1)

    def source(k, store):
        west_edge, east_edge = pltpu.roll(halo_t[...], 128 - k, 1), pltpu.roll(halo_t[...], 111 - k, 1)
        for r in range(4):
            at, rows = 8 + 32 * r, slice(32 * r, 32 * r + 32)
            f = fpad[k, at : at + 32, :]
            we, ee = west_edge[rows], east_edge[rows]
            west = jnp.where(lane2 == 0, jnp.concatenate([we, we], axis=1), pltpu.roll(f, 1, 1))
            east = jnp.where(lane2 == 255, jnp.concatenate([ee, ee], axis=1), pltpu.roll(f, 255, 1))
            up_down = fpad[k, at - 1 : at + 31, :] + fpad[k, at + 1 : at + 33, :]
            term = f + mlon[rows, :] * (west + east) + mlat[rows, :] * up_down
            store(rows, term * wlon[...])

    def to_lon(p, o):
        return remote(send1.at[p, o], got1.at[p, b], s1.at[p, o], r1.at[p, o], lon_peer(o))

    for p in range(2):

        def send_source(o, carry, p=p):
            d = lax.rem(b + o, 8)

            def store(rows, value):
                send1[p, o, rows, :] = value

            source(2 * d + p, store)
            to_lon(p, o).start()
            return carry

        lax.fori_loop(1, 8, send_source, 0)
    for p in range(2):

        def keep(rows, value, p=p):
            got1[p, b, rows, :] = value

        source(2 * b + p, keep)

    def basis_step(t, carry):
        for slot in range(4):
            i = t * 4 + slot
            basis_rows(i, slot).wait()

            def rows_split(r, c, slot=slot, i=i):
                high, lower = split(stage[slot, pl.ds(pl.multiple_of(r * 16, 16), 16), :])
                to = pl.ds(pl.multiple_of(i * 128 + r * 16, 16), 16)
                vh[to, :] = high
                vl[to, :] = lower
                return c

            lax.fori_loop(0, 8, rows_split, 0)

            @pl.when(t < 3)
            def _(i=i, slot=slot):
                basis_rows(i + 4, slot).start()

        return carry

    lax.fori_loop(0, 4, basis_step, 0)

    for c in coefs:
        c.wait()

    def at_step(g):
        return (pl.ds(g, 8, stride=STEPS), slice(None))

    ones, zeros = jnp.ones((8, 128), F32), jnp.zeros((8, 128), F32)

    for p in range(2):

        def coef_block(cb, carry, p=p):
            for t in range(TILES):
                c = cb * TILES + t
                scale = ones
                for g in range(STEPS):
                    scale = -low[(p, c, *at_step(g))] * scale
                    pref[(p, c, *at_step(g))] = scale
                total, _, enter, _ = segments_combined(scale, zeros, True)
                gc[core, chip, pl.ds(p * 48 + c, 1), :] = total[7:8]
                q, w = ones, zeros
                for g in range(STEPS)[::-1]:
                    at = (p, c, *at_step(g))
                    pivot = pinv[at]
                    u = -(up[at] * pivot)
                    up[at] = u
                    w = pivot * (pref[at] * enter) + u * w
                    q = u * q
                    qref[at] = q
                    wref[at] = w
                total_q, total_w, eq, ew = segments_combined(q, w, False)
                gc[core, chip, pl.ds(p * 48 + 16 + c, 1), :] = total_q[0:1]
                gc[core, chip, pl.ds(p * 48 + 32 + c, 1), :] = total_w[0:1]
                seg_eq[p, c] = eq
                seg_ew[p, c] = ew
            return carry

        lax.fori_loop(0, 16 // TILES, coef_block, 0)

    def coef_to(o):
        return remote(gc.at[core, chip], gc.at[core, chip], c_s.at[o], c_r.at[o], lat_peer(o))

    coef_pair = remote(gc.at[core], gc.at[core], c_s.at[0], c_r.at[0], partner)
    for o in range(1, 8):
        coef_to(o).start()

    def first_half(p):
        for o in range(1, 8):
            to_lon(p, o).wait_recv()

        def split_source(s, carry):
            high, lower = split(got1[p, s])
            cols = pl.ds(pl.multiple_of(s * 256, 256), 256)
            xh[:, cols] = high
            xl[:, cols] = lower
            return carry

        lax.fori_loop(0, 8, split_source, 0)

        def transform(n, carry):
            cols = pl.ds(pl.multiple_of(n * 512, 512), 512)
            block = product(xh[...], xl[...], vh[:, cols], vl[:, cols], NN)
            for t in range(4):
                body[p, n * 4 + t] = block[:, t * 128 : t * 128 + 128]
            return carry

        lax.fori_loop(0, 4, transform, 0)

        def solve_block(cb, carry):
            for t in range(TILES):
                c = cb * TILES + t
                x = zeros
                for g in range(STEPS):
                    at = (p, c, *at_step(g))
                    x = body[at] - low[at] * x
                    body[at] = x
                _, total, _, enter = segments_combined(pref[(p, c, *at_step(STEPS - 1))], x, True)
                gd[p, core, chip, pl.ds(c, 1), :] = total[7:8]
                y = zeros
                for g in range(STEPS)[::-1]:
                    at = (p, c, *at_step(g))
                    y = pinv[at] * (body[at] + pref[at] * enter) + up[at] * y
                    body[at] = y
                _, total, _, enter = segments_combined(qref[(p, c, *at_step(0))], y, False)
                gd[p, core, chip, pl.ds(16 + c, 1), :] = total[0:1]
                seg_eb[p, c] = enter
            return carry

        lax.fori_loop(0, 16 // TILES, solve_block, 0)
        for o in range(1, 8):
            data_to(p, o).start()

    def data_to(p, o):
        return remote(gd.at[p, core, chip], gd.at[p, core, chip], d_s.at[p, o], d_r.at[p, o], lat_peer(o))

    def data_pair(p):
        return remote(gd.at[p, core], gd.at[p, core], d_s.at[p, 0], d_r.at[p, 0], partner)

    def back_to(p, o):
        return remote(send2.at[p, o], out_h.at[2 * b + p], s2.at[p, o], r2.at[p, o], lon_peer(o))

    def second_half(p):
        for o in range(1, 8):
            data_to(p, o).wait_recv()
        data_pair(p).start()
        data_pair(p).wait_recv()
        entering, mine, entries = jnp.zeros((16, 128), F32), jnp.zeros((16, 128), F32), []
        for n in range(16):
            entries.append(entering)
            mine = jnp.where(a == n, entering, mine)
            entering = gc[n % 2, n // 2, p * 48 : p * 48 + 16, :] * entering + gd[p, n % 2, n // 2, 0:16, :]
        arriving, coming = jnp.zeros((16, 128), F32), jnp.zeros((16, 128), F32)
        for n in range(16)[::-1]:
            coming = jnp.where(a == n, arriving, coming)
            top = gd[p, n % 2, n // 2, 16:32, :] + gc[n % 2, n // 2, p * 48 + 32 : p * 48 + 48, :] * entries[n]
            arriving = gc[n % 2, n // 2, p * 48 + 16 : p * 48 + 32, :] * arriving + top
        for c in range(16):
            cols = slice(c * 128, c * 128 + 128)
            ent, arr = mine[c : c + 1], coming[c : c + 1]
            late = seg_eq[p, c] * arr + seg_eb[p, c] + seg_ew[p, c] * ent
            for s in range(8):
                rows = slice(s * 16, s * 16 + 16)
                value = body[p, c, rows] + wref[p, c, rows] * ent + qref[p, c, rows] * late[s : s + 1]
                high, lower = split(value)
                xh[rows, cols] = high
                xl[rows, cols] = lower

        def grid_block(o, carry):
            rows = pl.ds(pl.multiple_of(lax.rem(b + o, 8) * 256, 256), 256)
            send2[p, o] = product(xh[...], xl[...], vh[rows, :], vl[rows, :], NT)
            return carry

        def grid_send(o, carry):
            grid_block(o, carry)
            back_to(p, o).start()
            return carry

        lax.fori_loop(1, 8, grid_send, 0)
        grid_block(0, 0)
        own(p).start()

    def own(p):
        return copy(send2.at[p, 0], out_h.at[2 * b + p], l_own.at[p])

    first_half(0)
    for o in range(1, 8):
        coef_to(o).wait_recv()
    coef_pair.start()
    coef_pair.wait_recv()
    second_half(0)
    first_half(1)
    second_half(1)
    for o in range(1, 8):
        coef_to(o).wait_send()
    coef_pair.wait_send()
    for p in range(2):
        for o in range(1, 8):
            to_lon(p, o).wait_send()
            data_to(p, o).wait_send()
            back_to(p, o).wait_send()
        data_pair(p).wait_send()
        own(p).wait()
    for p in range(2):
        for o in range(1, 8):
            back_to(p, o).wait_recv()


def per_device(forcing, metric_lon, metric_lat, lon_weights, eigen_basis, lower_mult, pivot_inverse, upper_coef):
    vmem, dma = pltpu.VMEM, pltpu.SemaphoreType.DMA
    band = (2, 16, 128, 128)
    scratch = [
        vmem((16, 144, 256), F32), vmem((128, 256), F32), vmem((128, 256), F32), vmem((1, 256), F32),
        vmem((16, 256), F32), vmem((16, 256), F32), vmem((16, 256), F32), vmem((16, 256), F32),
        vmem((32, 128), F32), vmem((16, 128), F32), vmem((16, 128), F32), vmem((128, 128), F32),
        vmem((2, 8, 128, 256), F32), vmem((2, 8, 128, 256), F32), vmem((4, 128, 2048), F32),
        vmem((2048, 2048), BF16), vmem((2048, 2048), BF16),
        vmem(band, F32), vmem(band, F32), vmem(band, F32), vmem(band, F32), vmem(band, F32), vmem(band, F32),
        vmem((128, 2048), BF16), vmem((128, 2048), BF16), vmem(band, F32),
        vmem((2, 16, 8, 128), F32), vmem((2, 16, 8, 128), F32), vmem((2, 16, 8, 128), F32),
        vmem((2, 8, 96, 128), F32), vmem((2, 2, 8, 32, 128), F32), vmem((2, 8, 128, 256), F32),
        dma((4,)), dma((4,)), dma((3, 16)), dma((2,)), dma((4,)), dma((4,)), dma((2, 8)), dma((2, 8)),
        dma((8,)), dma((8,)), dma((2, 8)), dma((2, 8)), dma((2, 8)), dma((2, 8)),
    ]
    return pl.pallas_call(
        kernel,
        out_shape=jax.ShapeDtypeStruct((16, 128, 256), F32),
        in_specs=[pl.BlockSpec(memory_space=pl.ANY)] * 8,
        out_specs=pl.BlockSpec(memory_space=pl.ANY),
        scratch_shapes=scratch,
        compiler_params=pltpu.CompilerParams(collective_id=0, has_side_effects=True, vmem_limit_bytes=60 << 20),
    )(
        forcing, metric_lon, metric_lat, lon_weights.reshape(1, 256), eigen_basis,
        lower_mult, pivot_inverse, upper_coef,
    )


def solution(mesh):
    placed = (
        P(None, "lat", "lon"), P("lat", "lon"), P("lat", "lon"), P("lon"), P(),
        P("lon", "lat", None), P("lon", "lat", None), P("lon", "lat", None),
    )
    return jax.shard_map(
        per_device, mesh=mesh, in_specs=placed, out_specs=P(None, "lat", "lon"), check_vma=False
    )
```

time: 226 us -> 88.7 us (0.39); the launches traced: 222 us -> 88.5 us
  Pallas kernels: 0 us -> 85.4 us
  other arithmetic: 53.2 us -> 0 us
  matrix products: 44.6 us -> 0 us
  local copies, waits for them, and re-layouts: 36.1 us -> 3.1 us
  blocking collectives: 31.5 us -> 0 us
  starting transfers between devices: 30.9 us -> 0 us
  waiting for transfers between devices: 25.3 us -> 0 us
    pallas_call x0 -> x1, Pallas kernels: none -> 85.4 us  [per_device(): pl.pallas_call(kernel, out_shape=jax.ShapeDtypeStruct((16, 128, 256), F32...]
    dot_general x2 -> x0, matrix products: 44.6 us -> none  [the longest x1 27.4 us: per_device(): jnp.einsum('kjm,im->kji', modal, eigen_basis, precision=lax.Precision.HIG...]
    all_to_all x1 -> x0, blocking collectives: 31.5 us -> none  [per_device(): lax.all_to_all(on_grid, 'lon', split_axis=2, concat_axis=0, tiled=True)]
    all_to_all x3 -> x0, waiting for transfers between devices: 24.1 us -> none  [the longest x1 24.1 us: per_device(): lax.all_to_all(weighted, 'lon', split_axis=0, concat_axis=2, tiled=True)]
    unnamed x49 -> x0, other arithmetic: 20.7 us -> none
    all_to_all x3 -> x0, starting transfers between devices: 18.8 us -> none  [the longest x2 12.7 us: copy_for_each(): lax.all_to_all(jnp.broadcast_to(shard[None], (count, *shard.shape)), axis...]
    ppermute x4 -> x0, starting transfers between devices: 12.1 us -> none  [the longest x2 7.71 us: padded(): before = lax.ppermute(last, axis, up)]
    add x6 -> x0, other arithmetic: 11.2 us -> none  [the longest x2 8.31 us: band_recurrence(): local_shift + local_scale * group_shift]
  transfers between devices with their start and end apart: 7 -> 0, of which waited for: 3 -> 0; matrix products, arithmetic and copies ran while one was open for 19% -> 0% of each run, Pallas kernels for 0% -> 0%
where the time goes in v1:
time: 88.7 us; the launch traced here: 88.5 us
  Pallas kernels  85.4 us (96%)
  local copies, waits for them, and re-layouts  3.1 us (3%)
    pallas_call x1, Pallas kernels, per_device(): pl.pallas_call(kernel, out_shape=jax.ShapeDtypeStruct((16, 128, 256), F32...  85.4 us
    unnamed x1, local copies, waits for them, and re-layouts  3.1 us

profile of v1, /device:TPU:1, one launch (start us, length us, event | category | flops | bytes accessed | tf_op | source)
XLA Modules:
  0.0 88.5 jit_solution(15684266292304747515)
XLA Ops:
  0.0 85.4 %shard_map.82 = f32[16,128,256]{2,1,0:T(8,128)} custom-call(f32[16,128,256]{2,1,0:T(8,128)} %forcing_h.1, f32[128,256]{1,0:T(8,128)} %mlon_h.1, f32[128,256]{1,0:T(8,128)} %mlat_h.1, f32[1,256]{1,0:T(1,128)} %bitcast.1, f32[2048,2048]{1,0:T(8,128)} %basis_h.1, f32[2,128,2048]{2,1,0:T(8,128)} %low_h.1, f32[2,128,2048]{2,1,0:T(8,128)} %pinv_h.1, ...), custom_call_target="tpu_custom_call" | custom-call | tf_op jit(solution)/shard_map/pallas_call | solution.py:371
  85.4 3.1 %copy.10 = f32[16,128,256]{2,1,0:T(8,128)} copy(f32[16,128,256]{2,1,0:T(8,128)} %shard_map.82) | data formatting | bytes 4194304

commit v2 on v1

--- a/solution.py
+++ b/solution.py
@@ -13,6 +13,8 @@
 NT = (((1,), (1,)), ((), ()))
 TILES = 4
 STEPS = 16
+ORDER = (1, 3, 5, 7, 2, 4, 6)
+FIRST, BACK_FIRST = 64, 96
 
 
 def split(x):
@@ -20,9 +22,10 @@
     return high, (x - high.astype(F32)).astype(BF16)
 
 
-def product(lhs_high, lhs_low, rhs_high, rhs_low, dims):
+def product(pair, rhs_high, rhs_low, dims):
     dot = functools.partial(lax.dot_general, dimension_numbers=dims, preferred_element_type=F32)
-    return dot(lhs_high, rhs_high) + dot(lhs_high, rhs_low) + dot(lhs_low, rhs_high)
+    both = dot(pair, rhs_high)
+    return both[:128] + both[128:] + dot(pair[:128], rhs_low)
 
 
 def segments_combined(scale, shift, forward):
@@ -51,8 +54,10 @@
     forcing_h, mlon_h, mlat_h, wlon_h, basis_h, low_h, pinv_h, up_h, out_h,
     fpad, mlon, mlat, wlon, row_last, row_first, halo_n, halo_s, edge, halo_w, halo_e, halo_t,
     send1, got1, stage, vh, vl, low, pinv, up, pref, qref, wref,
-    xh, xl, body, seg_eq, seg_ew, seg_eb, gc, gd, send2,
+    pair, body, seg_eq, seg_ew, seg_eb, gc, gd, send2,
+    fix, fixes, fix_t,
     l_in, l_v, l_co, l_own, h_s, h_r, s1, r1, c_s, c_r, d_s, d_r, s2, r2,
+    f_s, f_r, late_s, late_r,
 ):
     a, b = lax.axis_index("lat"), lax.axis_index("lon")
     chip, core = lax.div(a, 2), lax.rem(a, 2)
@@ -90,19 +95,56 @@
     for peer in [lon_peer(o) for o in range(1, 8)] + [lat_peer(o) for o in range(1, 8)] + [north, south]:
         pl.semaphore_signal(barrier, inc=1, device_id=peer, device_id_type=MESH)
 
-    inputs[0].wait()
+    for c in inputs:
+        c.wait()
+    for c in coefs:
+        c.start()
     for slot in range(4):
         basis_rows(slot, slot).start()
-    for c in coefs:
-        c.start()
     lane = lax.broadcasted_iota(jnp.int32, (128, 128), 1)
-    columns = jnp.zeros((128, 128), F32)
+    lane2 = lax.broadcasted_iota(jnp.int32, (32, 256), 1)
+    columns = jnp.where(lane == 32, mlon[:, 0:1] * wlon[:, 0:1], 0.0)
+    columns = jnp.where(lane == 33, mlon[:, 255:256] * wlon[:, 255:256], columns)
+    nothing = jnp.zeros((1, 256), F32)
     for k in range(16):
         row_first[k : k + 1, :] = fpad[k, 8:9, :]
         row_last[k : k + 1, :] = fpad[k, 135:136, :]
         columns = jnp.where(lane == k, fpad[k, 8:136, 255:256], columns)
         columns = jnp.where(lane == 16 + k, fpad[k, 8:136, 0:1], columns)
-    edge[...] = columns.T[:32]
+        fpad[k, 7:8, :] = nothing
+        fpad[k, 136:137, :] = nothing
+    edge[...] = columns.T[:40]
+
+    def source(k, store, edges):
+        if edges:
+            west_edge, east_edge = pltpu.roll(halo_t[...], 128 - k, 1), pltpu.roll(halo_t[...], 111 - k, 1)
+        for r in range(4):
+            at, rows = 8 + 32 * r, slice(32 * r, 32 * r + 32)
+            f = fpad[k, at : at + 32, :]
+            we = jnp.concatenate([west_edge[rows]] * 2, axis=1) if edges else 0.0
+            ee = jnp.concatenate([east_edge[rows]] * 2, axis=1) if edges else 0.0
+            west = jnp.where(lane2 == 0, we, pltpu.roll(f, 1, 1))
+            east = jnp.where(lane2 == 255, ee, pltpu.roll(f, 255, 1))
+            up_down = fpad[k, at - 1 : at + 31, :] + fpad[k, at + 1 : at + 33, :]
+            term = f + mlon[rows, :] * (west + east) + mlat[rows, :] * up_down
+            store(rows, term * wlon[...])
+
+    def sources(p, edges):
+        def one(o, carry):
+            def store(rows, value):
+                send1[p, o, rows, :] = value
+
+            source(2 * lax.rem(b + o, 8) + p, store, edges)
+            return carry
+
+        lax.fori_loop(1, 8, one, 0)
+
+        def keep(rows, value):
+            got1[p, b, rows, :] = value
+
+        source(2 * b + p, keep, edges)
+
+    sources(0, False)
     pl.semaphore_wait(barrier, 16)
 
     def remote(src, dst, send, recv, peer):
@@ -118,51 +160,21 @@
     ]
     for c in halos:
         c.start()
-    for c in inputs[1:]:
-        c.wait()
-    for c in halos:
-        c.wait()
-    for k in range(16):
-        fpad[k, 7:8, :] = jnp.where(a > 0, halo_n[k : k + 1, :], 0.0)
-        fpad[k, 136:137, :] = jnp.where(a < 15, halo_s[k : k + 1, :], 0.0)
-    halo_t[...] = jnp.concatenate([halo_w[...], halo_e[...], jnp.zeros((96, 128), F32)], axis=0).T
-
-    lane2 = lax.broadcasted_iota(jnp.int32, (32, 256), 1)
-
-    def source(k, store):
-        west_edge, east_edge = pltpu.roll(halo_t[...], 128 - k, 1), pltpu.roll(halo_t[...], 111 - k, 1)
-        for r in range(4):
-            at, rows = 8 + 32 * r, slice(32 * r, 32 * r + 32)
-            f = fpad[k, at : at + 32, :]
-            we, ee = west_edge[rows], east_edge[rows]
-            west = jnp.where(lane2 == 0, jnp.concatenate([we, we], axis=1), pltpu.roll(f, 1, 1))
-            east = jnp.where(lane2 == 255, jnp.concatenate([ee, ee], axis=1), pltpu.roll(f, 255, 1))
-            up_down = fpad[k, at - 1 : at + 31, :] + fpad[k, at + 1 : at + 33, :]
-            term = f + mlon[rows, :] * (west + east) + mlat[rows, :] * up_down
-            store(rows, term * wlon[...])
 
     def to_lon(p, o):
-        return remote(send1.at[p, o], got1.at[p, b], s1.at[p, o], r1.at[p, o], lon_peer(o))
-
-    for p in range(2):
-
-        def send_source(o, carry, p=p):
-            d = lax.rem(b + o, 8)
-
-            def store(rows, value):
-                send1[p, o, rows, :] = value
-
-            source(2 * d + p, store)
-            to_lon(p, o).start()
-            return carry
-
-        lax.fori_loop(1, 8, send_source, 0)
-    for p in range(2):
-
-        def keep(rows, value, p=p):
-            got1[p, b, rows, :] = value
-
-        source(2 * b + p, keep)
+        rows = pl.ds(0, FIRST) if p == 1 and o % 2 else pl.ds(0, 128)
+        return remote(
+            send1.at[p, o, rows], got1.at[p, b, rows], s1.at[p, o], r1.at[p, o], lon_peer(o)
+        )
+
+    def to_lon_late(o):
+        rows = pl.ds(FIRST, 128 - FIRST)
+        return remote(
+            send1.at[1, o, rows], got1.at[1, b, rows], late_s.at[0, o], late_r.at[0, o], lon_peer(o)
+        )
+
+    for o in ORDER:
+        to_lon(0, o).start()
 
     def basis_step(t, carry):
         for slot in range(4):
@@ -184,19 +196,13 @@
 
         return carry
 
-    lax.fori_loop(0, 4, basis_step, 0)
-
-    for c in coefs:
-        c.wait()
-
     def at_step(g):
         return (pl.ds(g, 8, stride=STEPS), slice(None))
 
     ones, zeros = jnp.ones((8, 128), F32), jnp.zeros((8, 128), F32)
 
-    for p in range(2):
-
-        def coef_block(cb, carry, p=p):
+    def coefficients(p):
+        def coef_block(cb, carry):
             for t in range(TILES):
                 c = cb * TILES + t
                 scale = ones
@@ -204,7 +210,7 @@
                     scale = -low[(p, c, *at_step(g))] * scale
                     pref[(p, c, *at_step(g))] = scale
                 total, _, enter, _ = segments_combined(scale, zeros, True)
-                gc[core, chip, pl.ds(p * 48 + c, 1), :] = total[7:8]
+                gc[p, core, chip, pl.ds(c, 1), :] = total[7:8]
                 q, w = ones, zeros
                 for g in range(STEPS)[::-1]:
                     at = (p, c, *at_step(g))
@@ -216,37 +222,90 @@
                     qref[at] = q
                     wref[at] = w
                 total_q, total_w, eq, ew = segments_combined(q, w, False)
-                gc[core, chip, pl.ds(p * 48 + 16 + c, 1), :] = total_q[0:1]
-                gc[core, chip, pl.ds(p * 48 + 32 + c, 1), :] = total_w[0:1]
+                gc[p, core, chip, pl.ds(16 + c, 1), :] = total_q[0:1]
+                gc[p, core, chip, pl.ds(32 + c, 1), :] = total_w[0:1]
                 seg_eq[p, c] = eq
                 seg_ew[p, c] = ew
             return carry
 
         lax.fori_loop(0, 16 // TILES, coef_block, 0)
 
-    def coef_to(o):
-        return remote(gc.at[core, chip], gc.at[core, chip], c_s.at[o], c_r.at[o], lat_peer(o))
-
-    coef_pair = remote(gc.at[core], gc.at[core], c_s.at[0], c_r.at[0], partner)
+    def coef_to(p, o):
+        return remote(
+            gc.at[p, core, chip], gc.at[p, core, chip], c_s.at[p, o], c_r.at[p, o], lat_peer(o)
+        )
+
+    def coef_pair(p):
+        return remote(gc.at[p, core], gc.at[p, core], c_s.at[p, 0], c_r.at[p, 0], partner)
+
+    def fix_to(o):
+        return remote(fix.at[lax.rem(b + o, 8)], fixes.at[b], f_s.at[o], f_r.at[o], lon_peer(o))
+
+    for c in coefs:
+        c.wait()
+    coefficients(0)
     for o in range(1, 8):
-        coef_to(o).start()
+        coef_to(0, o).start()
+
+    for c in halos:
+        c.wait()
+    top = jnp.where(a > 0, halo_n[...], 0.0)
+    bottom = jnp.where(a < 15, halo_s[...], 0.0)
+    row_top, row_bottom = mlat[0:1, :] * top * wlon[...], mlat[127:128, :] * bottom * wlon[...]
+    col_left, col_right = halo_w[...] * edge[32:33, :], halo_e[...] * edge[33:34, :]
+    for d in range(8):
+        k = 2 * d
+        for i, row in enumerate((
+            row_top[k : k + 1, :128], row_top[k : k + 1, 128:], row_bottom[k : k + 1, :128],
+            row_bottom[k : k + 1, 128:], col_left[k : k + 1], col_right[k : k + 1],
+        )):
+            fix[d, i : i + 1, :] = row
+        fpad[k + 1, 7:8, :] = top[k + 1 : k + 2]
+        fpad[k + 1, 136:137, :] = bottom[k + 1 : k + 2]
+    for o in range(1, 8):
+        fix_to(o).start()
+    fixes[b, 0:6, :] = fix[b, 0:6, :]
+    halo_t[...] = jnp.concatenate([halo_w[...], halo_e[...], jnp.zeros((96, 128), F32)], axis=0).T
+    sources(1, True)
+    for o in ORDER:
+        to_lon(1, o).start()
+    lax.fori_loop(0, 4, basis_step, 0)
+    coefficients(1)
 
     def first_half(p):
         for o in range(1, 8):
             to_lon(p, o).wait_recv()
 
+        if p:
+            for o in range(1, 8, 2):
+                to_lon_late(o).wait_recv()
+        else:
+            for o in range(1, 8):
+                fix_to(o).wait_recv()
+            turned = [fixes[s, 4 + e : 5 + e, :] for e in range(2) for s in range(8)]
+            fix_t[...] = jnp.concatenate(turned + [jnp.zeros((112, 128), F32)], axis=0).T
+
         def split_source(s, carry):
-            high, lower = split(got1[p, s])
-            cols = pl.ds(pl.multiple_of(s * 256, 256), 256)
-            xh[:, cols] = high
-            xl[:, cols] = lower
+            for half in range(2):
+                lanes = slice(half * 128, half * 128 + 128)
+                value = got1[p, s, :, lanes]
+                if p == 0:
+                    row = lax.broadcasted_iota(jnp.int32, (128, 128), 0)
+                    column = pltpu.roll(fix_t[...], (119 if half else 128) - s, 1)
+                    value = value + jnp.where(lane == (127 if half else 0), column, 0.0)
+                    value = value + jnp.where(row == 0, fixes[s, half : half + 1, :], 0.0)
+                    value = value + jnp.where(row == 127, fixes[s, 2 + half : 3 + half, :], 0.0)
+                high, lower = split(value)
+                cols = pl.ds(pl.multiple_of(s * 256 + half * 128, 128), 128)
+                pair[0:128, cols] = high
+                pair[128:256, cols] = lower
             return carry
 
         lax.fori_loop(0, 8, split_source, 0)
 
         def transform(n, carry):
             cols = pl.ds(pl.multiple_of(n * 512, 512), 512)
-            block = product(xh[...], xl[...], vh[:, cols], vl[:, cols], NN)
+            block = product(pair[...], vh[:, cols], vl[:, cols], NN)
             for t in range(4):
                 body[p, n * 4 + t] = block[:, t * 128 : t * 128 + 128]
             return carry
@@ -283,8 +342,17 @@
     def data_pair(p):
         return remote(gd.at[p, core], gd.at[p, core], d_s.at[p, 0], d_r.at[p, 0], partner)
 
-    def back_to(p, o):
-        return remote(send2.at[p, o], out_h.at[2 * b + p], s2.at[p, o], r2.at[p, o], lon_peer(o))
+    def back_to(p, o, odd):
+        rows = pl.ds(0, BACK_FIRST) if p == 0 and odd else pl.ds(0, 128)
+        return remote(
+            send2.at[p, o, rows], out_h.at[2 * b + p, rows], s2.at[p, o], r2.at[p, o], lon_peer(o)
+        )
+
+    def back_late(o):
+        rows = pl.ds(BACK_FIRST, 128 - BACK_FIRST)
+        return remote(
+            send2.at[0, o, rows], out_h.at[2 * b, rows], late_s.at[1, o], late_r.at[1, o], lon_peer(o)
+        )
 
     def second_half(p):
         for o in range(1, 8):
@@ -295,12 +363,12 @@
         for n in range(16):
             entries.append(entering)
             mine = jnp.where(a == n, entering, mine)
-            entering = gc[n % 2, n // 2, p * 48 : p * 48 + 16, :] * entering + gd[p, n % 2, n // 2, 0:16, :]
+            entering = gc[p, n % 2, n // 2, 0:16, :] * entering + gd[p, n % 2, n // 2, 0:16, :]
         arriving, coming = jnp.zeros((16, 128), F32), jnp.zeros((16, 128), F32)
         for n in range(16)[::-1]:
             coming = jnp.where(a == n, arriving, coming)
-            top = gd[p, n % 2, n // 2, 16:32, :] + gc[n % 2, n // 2, p * 48 + 32 : p * 48 + 48, :] * entries[n]
-            arriving = gc[n % 2, n // 2, p * 48 + 16 : p * 48 + 32, :] * arriving + top
+            top = gd[p, n % 2, n // 2, 16:32, :] + gc[p, n % 2, n // 2, 32:48, :] * entries[n]
+            arriving = gc[p, n % 2, n // 2, 16:32, :] * arriving + top
         for c in range(16):
             cols = slice(c * 128, c * 128 + 128)
             ent, arr = mine[c : c + 1], coming[c : c + 1]
@@ -309,47 +377,69 @@
                 rows = slice(s * 16, s * 16 + 16)
                 value = body[p, c, rows] + wref[p, c, rows] * ent + qref[p, c, rows] * late[s : s + 1]
                 high, lower = split(value)
-                xh[rows, cols] = high
-                xl[rows, cols] = lower
-
-        def grid_block(o, carry):
+                pair[rows, cols] = high
+                pair[slice(128 + s * 16, 144 + s * 16), cols] = lower
+
+        def grid_block(o):
             rows = pl.ds(pl.multiple_of(lax.rem(b + o, 8) * 256, 256), 256)
-            send2[p, o] = product(xh[...], xl[...], vh[rows, :], vl[rows, :], NT)
-            return carry
-
-        def grid_send(o, carry):
-            grid_block(o, carry)
-            back_to(p, o).start()
-            return carry
-
-        lax.fori_loop(1, 8, grid_send, 0)
-        grid_block(0, 0)
+            send2[p, o] = product(pair[...], vh[rows, :], vl[rows, :], NT)
+
+        def odd_block(t, carry):
+            o = 2 * t + 1
+            grid_block(o)
+            back_to(p, o, True).start()
+            return carry
+
+        def even_block(t, carry):
+            o = 2 * t
+            grid_block(o)
+            back_to(p, o, False).start()
+            return carry
+
+        lax.fori_loop(0, 4, odd_block, 0)
+        lax.fori_loop(1, 4, even_block, 0)
+        grid_block(0)
         own(p).start()
 
     def own(p):
         return copy(send2.at[p, 0], out_h.at[2 * b + p], l_own.at[p])
 
+    def coef_forward(p):
+        for o in range(1, 8):
+            coef_to(p, o).wait_recv()
+        coef_pair(p).start()
+        coef_pair(p).wait_recv()
+
     first_half(0)
+    for o in range(1, 8, 2):
+        to_lon_late(o).start()
     for o in range(1, 8):
-        coef_to(o).wait_recv()
-    coef_pair.start()
-    coef_pair.wait_recv()
+        coef_to(1, o).start()
+    coef_forward(0)
     second_half(0)
     first_half(1)
+    for o in range(1, 8, 2):
+        back_late(o).start()
+    coef_forward(1)
     second_half(1)
-    for o in range(1, 8):
-        coef_to(o).wait_send()
-    coef_pair.wait_send()
     for p in range(2):
         for o in range(1, 8):
+            coef_to(p, o).wait_send()
             to_lon(p, o).wait_send()
             data_to(p, o).wait_send()
-            back_to(p, o).wait_send()
+            back_to(p, o, o % 2).wait_send()
+        coef_pair(p).wait_send()
         data_pair(p).wait_send()
         own(p).wait()
+    for o in range(1, 8):
+        fix_to(o).wait_send()
+    for o in range(1, 8, 2):
+        to_lon_late(o).wait_send()
+        back_late(o).wait_send()
+        back_late(o).wait_recv()
     for p in range(2):
         for o in range(1, 8):
-            back_to(p, o).wait_recv()
+            back_to(p, o, o % 2).wait_recv()
 
 
 def per_device(forcing, metric_lon, metric_lat, lon_weights, eigen_basis, lower_mult, pivot_inverse, upper_coef):
@@ -358,15 +448,17 @@
     scratch = [
         vmem((16, 144, 256), F32), vmem((128, 256), F32), vmem((128, 256), F32), vmem((1, 256), F32),
         vmem((16, 256), F32), vmem((16, 256), F32), vmem((16, 256), F32), vmem((16, 256), F32),
-        vmem((32, 128), F32), vmem((16, 128), F32), vmem((16, 128), F32), vmem((128, 128), F32),
+        vmem((40, 128), F32), vmem((16, 128), F32), vmem((16, 128), F32), vmem((128, 128), F32),
         vmem((2, 8, 128, 256), F32), vmem((2, 8, 128, 256), F32), vmem((4, 128, 2048), F32),
         vmem((2048, 2048), BF16), vmem((2048, 2048), BF16),
         vmem(band, F32), vmem(band, F32), vmem(band, F32), vmem(band, F32), vmem(band, F32), vmem(band, F32),
-        vmem((128, 2048), BF16), vmem((128, 2048), BF16), vmem(band, F32),
+        vmem((256, 2048), BF16), vmem(band, F32),
         vmem((2, 16, 8, 128), F32), vmem((2, 16, 8, 128), F32), vmem((2, 16, 8, 128), F32),
-        vmem((2, 8, 96, 128), F32), vmem((2, 2, 8, 32, 128), F32), vmem((2, 8, 128, 256), F32),
+        vmem((2, 2, 8, 48, 128), F32), vmem((2, 2, 8, 32, 128), F32), vmem((2, 8, 128, 256), F32),
+        vmem((8, 8, 128), F32), vmem((8, 8, 128), F32), vmem((128, 128), F32),
         dma((4,)), dma((4,)), dma((3, 16)), dma((2,)), dma((4,)), dma((4,)), dma((2, 8)), dma((2, 8)),
-        dma((8,)), dma((8,)), dma((2, 8)), dma((2, 8)), dma((2, 8)), dma((2, 8)),
+        dma((2, 8)), dma((2, 8)), dma((2, 8)), dma((2, 8)), dma((2, 8)), dma((2, 8)),
+        dma((8,)), dma((8,)), dma((2, 8)), dma((2, 8)),
     ]
     return pl.pallas_call(
         kernel,

time: 88.7 us -> 81 us (0.913)
  Pallas kernels: 85.4 us -> 77.7 us
    pallas_call x1, Pallas kernels: 85.4 us -> 77.7 us  [per_device(): pl.pallas_call(kernel, out_shape=jax.ShapeDtypeStruct((16, 128, 256), F32...]
where the time goes in v2:
time: 81 us; the launch traced here: 80.8 us
  Pallas kernels  77.7 us (96%)
  local copies, waits for them, and re-layouts  3.1 us (4%)
    pallas_call x1, Pallas kernels, per_device(): pl.pallas_call(kernel, out_shape=jax.ShapeDtypeStruct((16, 128, 256), F32...  77.7 us
    unnamed x1, local copies, waits for them, and re-layouts  3.1 us

profile of v2, /device:TPU:1, one launch (start us, length us, event | category | flops | bytes accessed | tf_op | source)
XLA Modules:
  0.0 80.8 jit_solution(6012164557316784624)
XLA Ops:
  0.0 77.7 %shard_map.82 = f32[16,128,256]{2,1,0:T(8,128)} custom-call(f32[16,128,256]{2,1,0:T(8,128)} %forcing_h.1, f32[128,256]{1,0:T(8,128)} %mlon_h.1, f32[128,256]{1,0:T(8,128)} %mlat_h.1, f32[1,256]{1,0:T(1,128)} %bitcast.1, f32[2048,2048]{1,0:T(8,128)} %basis_h.1, f32[2,128,2048]{2,1,0:T(8,128)} %low_h.1, f32[2,128,2048]{2,1,0:T(8,128)} %pinv_h.1, ...), custom_call_target="tpu_custom_call" | custom-call | tf_op jit(solution)/shard_map/pallas_call | solution.py:463
  77.7 3.1 %copy.10 = f32[16,128,256]{2,1,0:T(8,128)} copy(f32[16,128,256]{2,1,0:T(8,128)} %shard_map.82) | data formatting | bytes 4194304

commit v3 on v2

--- a/solution.py
+++ b/solution.py
@@ -13,8 +13,8 @@
 NT = (((1,), (1,)), ((), ()))
 TILES = 4
 STEPS = 16
-ORDER = (1, 3, 5, 7, 2, 4, 6)
-FIRST, BACK_FIRST = 64, 96
+ORDER = (1, 3, 2, 4, 6, 5, 7)
+FIRST, BACK_FIRST = 64, 64
 
 
 def split(x):
@@ -51,13 +51,13 @@
 
 
 def kernel(
-    forcing_h, mlon_h, mlat_h, wlon_h, basis_h, low_h, pinv_h, up_h, out_h,
+    forcing_h, mlon_h, mlat_h, wlon_h, basis_h, low_h, pinv_h, up_h, out,
     fpad, mlon, mlat, wlon, row_last, row_first, halo_n, halo_s, edge, halo_w, halo_e, halo_t,
     send1, got1, stage, vh, vl, low, pinv, up, pref, qref, wref,
-    pair, body, seg_eq, seg_ew, seg_eb, gc, gd, send2,
+    pair, modal, body, seg_eq, seg_ew, seg_eb, gc, gd, send2,
     fix, fixes, fix_t,
     l_in, l_v, l_co, l_own, h_s, h_r, s1, r1, c_s, c_r, d_s, d_r, s2, r2,
-    f_s, f_r, late_s, late_r,
+    f_s, f_r, late_s, late_r, g_s, g_r,
 ):
     a, b = lax.axis_index("lat"), lax.axis_index("lon")
     chip, core = lax.div(a, 2), lax.rem(a, 2)
@@ -85,8 +85,16 @@
     def lon_peer(o):
         return {"lon": lax.rem(b + o, 8)}
 
+    x_lo, z = lax.div(chip, 4), lax.rem(chip, 4)
+
     def lat_peer(o):
-        return {"lat": lax.rem(chip + o, 8) * 2 + core}
+        return {"lat": (lax.rem(x_lo + o // 4, 2) * 4 + lax.rem(z + o % 4, 4)) * 2 + core}
+
+    def lat_from(o):
+        return lax.rem(x_lo + o // 4, 2) * 4 + lax.rem(z + 4 - o % 4, 4)
+
+    def place(sector):
+        return pl.multiple_of(lax.rem(sector, 2) * 1024 + lax.div(sector, 2) * 256, 256)
 
     partner = {"lat": chip * 2 + 1 - core}
     north, south = {"lat": lax.rem(a + 15, 16)}, {"lat": lax.rem(a + 1, 16)}
@@ -173,7 +181,7 @@
             send1.at[1, o, rows], got1.at[1, b, rows], late_s.at[0, o], late_r.at[0, o], lon_peer(o)
         )
 
-    for o in ORDER:
+    for o in ORDER[:5]:
         to_lon(0, o).start()
 
     def basis_step(t, carry):
@@ -183,7 +191,8 @@
 
             def rows_split(r, c, slot=slot, i=i):
                 high, lower = split(stage[slot, pl.ds(pl.multiple_of(r * 16, 16), 16), :])
-                to = pl.ds(pl.multiple_of(i * 128 + r * 16, 16), 16)
+                base = place(lax.div(i, 2)) + lax.rem(i, 2) * 128
+                to = pl.ds(pl.multiple_of(base + r * 16, 16), 16)
                 vh[to, :] = high
                 vl[to, :] = lower
                 return c
@@ -235,6 +244,12 @@
             gc.at[p, core, chip], gc.at[p, core, chip], c_s.at[p, o], c_r.at[p, o], lat_peer(o)
         )
 
+    def coef_on(p, o):
+        other = lat_from(4)
+        return remote(
+            gc.at[p, core, other], gc.at[p, core, other], c_s.at[p, 4 + o], c_r.at[p, 4 + o], lat_peer(o)
+        )
+
     def coef_pair(p):
         return remote(gc.at[p, core], gc.at[p, core], c_s.at[p, 0], c_r.at[p, 0], partner)
 
@@ -244,8 +259,11 @@
     for c in coefs:
         c.wait()
     coefficients(0)
-    for o in range(1, 8):
+    for o in range(1, 5):
         coef_to(0, o).start()
+    for o in ORDER[5:]:
+        to_lon(0, o).start()
+    lax.fori_loop(0, 4, basis_step, 0)
 
     for c in halos:
         c.wait()
@@ -269,48 +287,59 @@
     sources(1, True)
     for o in ORDER:
         to_lon(1, o).start()
-    lax.fori_loop(0, 4, basis_step, 0)
+    coef_to(0, 4).wait_recv()
+    for o in range(1, 4):
+        coef_on(0, o).start()
     coefficients(1)
-
-    def first_half(p):
-        for o in range(1, 8):
+    for o in range(1, 5):
+        coef_to(1, o).start()
+
+    def transform(p, part):
+        parity = lax.rem(b + part, 2)
+        for o in range(2 - part, 8, 2):
             to_lon(p, o).wait_recv()
-
-        if p:
-            for o in range(1, 8, 2):
+            if p == 0:
+                fix_to(o).wait_recv()
+            elif part:
                 to_lon_late(o).wait_recv()
-        else:
-            for o in range(1, 8):
-                fix_to(o).wait_recv()
-            turned = [fixes[s, 4 + e : 5 + e, :] for e in range(2) for s in range(8)]
-            fix_t[...] = jnp.concatenate(turned + [jnp.zeros((112, 128), F32)], axis=0).T
-
-        def split_source(s, carry):
+        if p == 0:
+            turned = [fixes[2 * t + parity, 4 + e : 5 + e, :] for e in range(2) for t in range(4)]
+            fix_t[...] = jnp.concatenate(turned + [jnp.zeros((120, 128), F32)], axis=0).T
+
+        def split_source(t, carry):
+            s = 2 * t + parity
             for half in range(2):
-                lanes = slice(half * 128, half * 128 + 128)
-                value = got1[p, s, :, lanes]
+                value = got1[p, s, :, half * 128 : half * 128 + 128]
                 if p == 0:
                     row = lax.broadcasted_iota(jnp.int32, (128, 128), 0)
-                    column = pltpu.roll(fix_t[...], (119 if half else 128) - s, 1)
+                    column = pltpu.roll(fix_t[...], (123 if half else 128) - t, 1)
                     value = value + jnp.where(lane == (127 if half else 0), column, 0.0)
                     value = value + jnp.where(row == 0, fixes[s, half : half + 1, :], 0.0)
                     value = value + jnp.where(row == 127, fixes[s, 2 + half : 3 + half, :], 0.0)
                 high, lower = split(value)
-                cols = pl.ds(pl.multiple_of(s * 256 + half * 128, 128), 128)
+                cols = pl.ds(pl.multiple_of(place(s) + half * 128, 128), 128)
                 pair[0:128, cols] = high
                 pair[128:256, cols] = lower
             return carry
 
-        lax.fori_loop(0, 8, split_source, 0)
-
-        def transform(n, carry):
+        lax.fori_loop(0, 4, split_source, 0)
+        depth = pl.ds(pl.multiple_of(parity * 1024, 1024), 1024)
+
+        def columns_of(n, carry):
             cols = pl.ds(pl.multiple_of(n * 512, 512), 512)
-            block = product(pair[...], vh[:, cols], vl[:, cols], NN)
+            block = product(pair[:, depth], vh[depth, cols], vl[depth, cols], NN)
             for t in range(4):
-                body[p, n * 4 + t] = block[:, t * 128 : t * 128 + 128]
-            return carry
-
-        lax.fori_loop(0, 4, transform, 0)
+                tile = block[:, t * 128 : t * 128 + 128]
+                body[p, n * 4 + t] = body[p, n * 4 + t] + tile if part else tile
+            return carry
+
+        lax.fori_loop(0, 4, columns_of, 0)
+
+    def solve(p):
+        for o in range(1, 4):
+            coef_to(p, o).wait_recv()
+            coef_on(p, o).wait_recv()
+        coef_pair(p).start()
 
         def solve_block(cb, carry):
             for t in range(TILES):
@@ -335,30 +364,34 @@
         lax.fori_loop(0, 16 // TILES, solve_block, 0)
         for o in range(1, 8):
             data_to(p, o).start()
+        data_pair(p, 0).start()
 
     def data_to(p, o):
         return remote(gd.at[p, core, chip], gd.at[p, core, chip], d_s.at[p, o], d_r.at[p, o], lat_peer(o))
 
-    def data_pair(p):
-        return remote(gd.at[p, core], gd.at[p, core], d_s.at[p, 0], d_r.at[p, 0], partner)
+    def data_pair(p, o):
+        slot = gd.at[p, core, lat_from(o)]
+        return remote(slot, slot, g_s.at[p, o], g_r.at[p, o], partner)
 
     def back_to(p, o, odd):
         rows = pl.ds(0, BACK_FIRST) if p == 0 and odd else pl.ds(0, 128)
         return remote(
-            send2.at[p, o, rows], out_h.at[2 * b + p, rows], s2.at[p, o], r2.at[p, o], lon_peer(o)
+            send2.at[p, o, rows], out.at[2 * b + p, rows], s2.at[p, o], r2.at[p, o], lon_peer(o)
         )
 
     def back_late(o):
         rows = pl.ds(BACK_FIRST, 128 - BACK_FIRST)
         return remote(
-            send2.at[0, o, rows], out_h.at[2 * b, rows], late_s.at[1, o], late_r.at[1, o], lon_peer(o)
-        )
-
-    def second_half(p):
+            send2.at[0, o, rows], out.at[2 * b, rows], late_s.at[1, o], late_r.at[1, o], lon_peer(o)
+        )
+
+    def carries(p):
         for o in range(1, 8):
             data_to(p, o).wait_recv()
-        data_pair(p).start()
-        data_pair(p).wait_recv()
+            data_pair(p, o).start()
+        coef_pair(p).wait_recv()
+        for o in range(8):
+            data_pair(p, o).wait_recv()
         entering, mine, entries = jnp.zeros((16, 128), F32), jnp.zeros((16, 128), F32), []
         for n in range(16):
             entries.append(entering)
@@ -377,59 +410,65 @@
                 rows = slice(s * 16, s * 16 + 16)
                 value = body[p, c, rows] + wref[p, c, rows] * ent + qref[p, c, rows] * late[s : s + 1]
                 high, lower = split(value)
-                pair[rows, cols] = high
-                pair[slice(128 + s * 16, 144 + s * 16), cols] = lower
-
-        def grid_block(o):
-            rows = pl.ds(pl.multiple_of(lax.rem(b + o, 8) * 256, 256), 256)
-            send2[p, o] = product(pair[...], vh[rows, :], vl[rows, :], NT)
-
-        def odd_block(t, carry):
-            o = 2 * t + 1
-            grid_block(o)
-            back_to(p, o, True).start()
-            return carry
-
-        def even_block(t, carry):
-            o = 2 * t
-            grid_block(o)
-            back_to(p, o, False).start()
-            return carry
-
-        lax.fori_loop(0, 4, odd_block, 0)
-        lax.fori_loop(1, 4, even_block, 0)
-        grid_block(0)
+                modal[rows, cols] = high
+                modal[slice(128 + s * 16, 144 + s * 16), cols] = lower
+
+    def grid_block(p, o):
+        rows = pl.ds(place(lax.rem(b + o, 8)), 256)
+        send2[p, o] = product(modal[...], vh[rows, :], vl[rows, :], NT)
+
+    def across(p):
+        def block(t, carry):
+            grid_block(p, 2 * t + 1)
+            back_to(p, 2 * t + 1, True).start()
+            return carry
+
+        lax.fori_loop(0, 4, block, 0)
+
+    def along(p):
+        def block(t, carry):
+            grid_block(p, 2 * t)
+            back_to(p, 2 * t, False).start()
+            return carry
+
+        lax.fori_loop(1, 4, block, 0)
+        grid_block(p, 0)
         own(p).start()
 
     def own(p):
-        return copy(send2.at[p, 0], out_h.at[2 * b + p], l_own.at[p])
-
-    def coef_forward(p):
-        for o in range(1, 8):
-            coef_to(p, o).wait_recv()
-        coef_pair(p).start()
-        coef_pair(p).wait_recv()
-
-    first_half(0)
+        return copy(send2.at[p, 0], out.at[2 * b + p], l_own.at[p])
+
+    transform(0, 0)
+    transform(0, 1)
+    solve(0)
     for o in range(1, 8, 2):
         to_lon_late(o).start()
-    for o in range(1, 8):
-        coef_to(1, o).start()
-    coef_forward(0)
-    second_half(0)
-    first_half(1)
+    transform(1, 0)
+    coef_to(1, 4).wait_recv()
+    for o in range(1, 4):
+        coef_on(1, o).start()
+    carries(0)
+    across(0)
+    transform(1, 1)
+    solve(1)
     for o in range(1, 8, 2):
         back_late(o).start()
-    coef_forward(1)
-    second_half(1)
+    along(0)
+    carries(1)
+    across(1)
+    along(1)
     for p in range(2):
+        for o in range(1, 5):
+            coef_to(p, o).wait_send()
+        for o in range(1, 4):
+            coef_on(p, o).wait_send()
+        data_pair(p, 0).wait_send()
         for o in range(1, 8):
-            coef_to(p, o).wait_send()
+            data_pair(p, o).wait_send()
             to_lon(p, o).wait_send()
             data_to(p, o).wait_send()
             back_to(p, o, o % 2).wait_send()
         coef_pair(p).wait_send()
-        data_pair(p).wait_send()
         own(p).wait()
     for o in range(1, 8):
         fix_to(o).wait_send()
@@ -452,19 +491,19 @@
         vmem((2, 8, 128, 256), F32), vmem((2, 8, 128, 256), F32), vmem((4, 128, 2048), F32),
         vmem((2048, 2048), BF16), vmem((2048, 2048), BF16),
         vmem(band, F32), vmem(band, F32), vmem(band, F32), vmem(band, F32), vmem(band, F32), vmem(band, F32),
-        vmem((256, 2048), BF16), vmem(band, F32),
+        vmem((256, 2048), BF16), vmem((256, 2048), BF16), vmem(band, F32),
         vmem((2, 16, 8, 128), F32), vmem((2, 16, 8, 128), F32), vmem((2, 16, 8, 128), F32),
         vmem((2, 2, 8, 48, 128), F32), vmem((2, 2, 8, 32, 128), F32), vmem((2, 8, 128, 256), F32),
         vmem((8, 8, 128), F32), vmem((8, 8, 128), F32), vmem((128, 128), F32),
         dma((4,)), dma((4,)), dma((3, 16)), dma((2,)), dma((4,)), dma((4,)), dma((2, 8)), dma((2, 8)),
         dma((2, 8)), dma((2, 8)), dma((2, 8)), dma((2, 8)), dma((2, 8)), dma((2, 8)),
-        dma((8,)), dma((8,)), dma((2, 8)), dma((2, 8)),
+        dma((8,)), dma((8,)), dma((2, 8)), dma((2, 8)), dma((2, 8)), dma((2, 8)),
     ]
     return pl.pallas_call(
         kernel,
-        out_shape=jax.ShapeDtypeStruct((16, 128, 256), F32),
+        out_shape=pltpu.VMEM((16, 128, 256), F32),
         in_specs=[pl.BlockSpec(memory_space=pl.ANY)] * 8,
-        out_specs=pl.BlockSpec(memory_space=pl.ANY),
+        out_specs=pl.BlockSpec(memory_space=pltpu.VMEM),
         scratch_shapes=scratch,
         compiler_params=pltpu.CompilerParams(collective_id=0, has_side_effects=True, vmem_limit_bytes=60 << 20),
     )(

time: 81 us -> 73 us (0.901)
  Pallas kernels: 77.7 us -> 71.5 us
  local copies, waits for them, and re-layouts: 3.1 us -> 1.32 us
    pallas_call x1, Pallas kernels: 77.7 us -> 71.5 us  [per_device(): pl.pallas_call(kernel, out_shape=pltpu.VMEM((16, 128, 256), F32), in_spec...]
    unnamed x1, local copies, waits for them, and re-layouts: 3.1 us -> 1.32 us
where the time goes in v3:
time: 73 us; the launch traced here: 72.9 us
  Pallas kernels  71.5 us (98%)
  local copies, waits for them, and re-layouts  1.32 us (2%)
    pallas_call x1, Pallas kernels, per_device(): pl.pallas_call(kernel, out_shape=pltpu.VMEM((16, 128, 256), F32), in_spec...  71.5 us

profile of v3, /device:TPU:1, one launch (start us, length us, event | category | flops | bytes accessed | tf_op | source)
XLA Modules:
  0.0 72.9 jit_solution(16456363898195899866)
XLA Ops:
  0.0 71.5 %shard_map.82 = f32[16,128,256]{2,1,0:T(8,128)S(1)} custom-call(f32[16,128,256]{2,1,0:T(8,128)} %forcing_h.1, f32[128,256]{1,0:T(8,128)} %mlon_h.1, f32[128,256]{1,0:T(8,128)} %mlat_h.1, f32[1,256]{1,0:T(1,128)} %bitcast.1, f32[2048,2048]{1,0:T(8,128)} %basis_h.1, f32[2,128,2048]{2,1,0:T(8,128)} %low_h.1, f32[2,128,2048]{2,1,0:T(8,128)} %pinv_h.1, ...), custom_call_target="tpu_custom_call" | custom-call | tf_op jit(solution)/shard_map/pallas_call | solution.py:502
  71.6 1.3 %copy.10 = f32[16,128,256]{2,1,0:T(8,128)} copy(f32[16,128,256]{2,1,0:T(8,128)S(1)} %shard_map.82) | data formatting | bytes 4194304

commit v4 on v3

--- a/solution.py
+++ b/solution.py
@@ -14,7 +14,7 @@
 TILES = 4
 STEPS = 16
 ORDER = (1, 3, 2, 4, 6, 5, 7)
-FIRST, BACK_FIRST = 64, 64
+FIRST = 96
 
 
 def split(x):
@@ -82,8 +82,14 @@
         for c in range(16)
     ]
 
+    def lon_id(o):
+        y = lax.div(b, 2)
+        along_y = lax.rem(y + lax.div(o, 2), 4) * 2 + lax.rem(b, 2)
+        across_x = lax.rem(y + 2 + 3 * lax.div(o, 2), 4) * 2 + 1 - lax.rem(b, 2)
+        return jnp.where(lax.rem(o, 2) == 1, across_x, along_y)
+
     def lon_peer(o):
-        return {"lon": lax.rem(b + o, 8)}
+        return {"lon": lon_id(o)}
 
     x_lo, z = lax.div(chip, 4), lax.rem(chip, 4)
 
@@ -142,7 +148,7 @@
             def store(rows, value):
                 send1[p, o, rows, :] = value
 
-            source(2 * lax.rem(b + o, 8) + p, store, edges)
+            source(2 * lon_id(o) + p, store, edges)
             return carry
 
         lax.fori_loop(1, 8, one, 0)
@@ -161,8 +167,8 @@
         )
 
     halos = [
-        remote(edge.at[pl.ds(0, 16)], halo_w, h_s.at[0], h_r.at[0], lon_peer(1)),
-        remote(edge.at[pl.ds(16, 16)], halo_e, h_s.at[1], h_r.at[1], lon_peer(7)),
+        remote(edge.at[pl.ds(0, 16)], halo_w, h_s.at[0], h_r.at[0], {"lon": lax.rem(b + 1, 8)}),
+        remote(edge.at[pl.ds(16, 16)], halo_e, h_s.at[1], h_r.at[1], {"lon": lax.rem(b + 7, 8)}),
         remote(row_last, halo_n, h_s.at[2], h_r.at[2], south),
         remote(row_first, halo_s, h_s.at[3], h_r.at[3], north),
     ]
@@ -178,7 +184,7 @@
     def to_lon_late(o):
         rows = pl.ds(FIRST, 128 - FIRST)
         return remote(
-            send1.at[1, o, rows], got1.at[1, b, rows], late_s.at[0, o], late_r.at[0, o], lon_peer(o)
+            send1.at[1, o, rows], got1.at[1, b, rows], late_s.at[o], late_r.at[o], lon_peer(o)
         )
 
     for o in ORDER[:5]:
@@ -254,7 +260,7 @@
         return remote(gc.at[p, core], gc.at[p, core], c_s.at[p, 0], c_r.at[p, 0], partner)
 
     def fix_to(o):
-        return remote(fix.at[lax.rem(b + o, 8)], fixes.at[b], f_s.at[o], f_r.at[o], lon_peer(o))
+        return remote(fix.at[lon_id(o)], fixes.at[b], f_s.at[o], f_r.at[o], lon_peer(o))
 
     for c in coefs:
         c.wait()
@@ -341,7 +347,7 @@
             coef_on(p, o).wait_recv()
         coef_pair(p).start()
 
-        def solve_block(cb, carry):
+        def forward_block(cb, carry):
             for t in range(TILES):
                 c = cb * TILES + t
                 x = zeros
@@ -350,57 +356,65 @@
                     x = body[at] - low[at] * x
                     body[at] = x
                 _, total, _, enter = segments_combined(pref[(p, c, *at_step(STEPS - 1))], x, True)
-                gd[p, core, chip, pl.ds(c, 1), :] = total[7:8]
+                gd[p, 0, core, chip, pl.ds(c, 1), :] = total[7:8]
+                seg_eb[p, c] = enter
+            return carry
+
+        lax.fori_loop(0, 16 // TILES, forward_block, 0)
+        for o in range(1, 8):
+            data_to(p, 0, o).start()
+        data_pair(p, 0, 0).start()
+
+        def backward_block(cb, carry):
+            for t in range(TILES):
+                c = cb * TILES + t
+                enter = seg_eb[p, c]
                 y = zeros
                 for g in range(STEPS)[::-1]:
                     at = (p, c, *at_step(g))
                     y = pinv[at] * (body[at] + pref[at] * enter) + up[at] * y
                     body[at] = y
                 _, total, _, enter = segments_combined(qref[(p, c, *at_step(0))], y, False)
-                gd[p, core, chip, pl.ds(16 + c, 1), :] = total[0:1]
+                gd[p, 1, core, chip, pl.ds(c, 1), :] = total[0:1]
                 seg_eb[p, c] = enter
             return carry
 
-        lax.fori_loop(0, 16 // TILES, solve_block, 0)
+        lax.fori_loop(0, 16 // TILES, backward_block, 0)
         for o in range(1, 8):
-            data_to(p, o).start()
-        data_pair(p, 0).start()
-
-    def data_to(p, o):
-        return remote(gd.at[p, core, chip], gd.at[p, core, chip], d_s.at[p, o], d_r.at[p, o], lat_peer(o))
-
-    def data_pair(p, o):
-        slot = gd.at[p, core, lat_from(o)]
-        return remote(slot, slot, g_s.at[p, o], g_r.at[p, o], partner)
-
-    def back_to(p, o, odd):
-        rows = pl.ds(0, BACK_FIRST) if p == 0 and odd else pl.ds(0, 128)
+            data_to(p, 1, o).start()
+        data_pair(p, 1, 0).start()
+
+    def data_to(p, i, o):
+        slot = gd.at[p, i, core, chip]
+        return remote(slot, slot, d_s.at[p, i, o], d_r.at[p, i, o], lat_peer(o))
+
+    def data_pair(p, i, o):
+        slot = gd.at[p, i, core, lat_from(o)]
+        return remote(slot, slot, g_s.at[p, i, o], g_r.at[p, i, o], partner)
+
+    def back_to(p, o):
         return remote(
-            send2.at[p, o, rows], out.at[2 * b + p, rows], s2.at[p, o], r2.at[p, o], lon_peer(o)
+            send2.at[p, o], out.at[2 * b + p], s2.at[p, o], r2.at[p, o], lon_peer(o)
         )
 
-    def back_late(o):
-        rows = pl.ds(BACK_FIRST, 128 - BACK_FIRST)
-        return remote(
-            send2.at[0, o, rows], out.at[2 * b, rows], late_s.at[1, o], late_r.at[1, o], lon_peer(o)
-        )
-
     def carries(p):
-        for o in range(1, 8):
-            data_to(p, o).wait_recv()
-            data_pair(p, o).start()
+        for i in range(2):
+            for o in range(1, 8):
+                data_to(p, i, o).wait_recv()
+                data_pair(p, i, o).start()
         coef_pair(p).wait_recv()
-        for o in range(8):
-            data_pair(p, o).wait_recv()
+        for i in range(2):
+            for o in range(8):
+                data_pair(p, i, o).wait_recv()
         entering, mine, entries = jnp.zeros((16, 128), F32), jnp.zeros((16, 128), F32), []
         for n in range(16):
             entries.append(entering)
             mine = jnp.where(a == n, entering, mine)
-            entering = gc[p, n % 2, n // 2, 0:16, :] * entering + gd[p, n % 2, n // 2, 0:16, :]
+            entering = gc[p, n % 2, n // 2, 0:16, :] * entering + gd[p, 0, n % 2, n // 2]
         arriving, coming = jnp.zeros((16, 128), F32), jnp.zeros((16, 128), F32)
         for n in range(16)[::-1]:
             coming = jnp.where(a == n, arriving, coming)
-            top = gd[p, n % 2, n // 2, 16:32, :] + gc[p, n % 2, n // 2, 32:48, :] * entries[n]
+            top = gd[p, 1, n % 2, n // 2] + gc[p, n % 2, n // 2, 32:48, :] * entries[n]
             arriving = gc[p, n % 2, n // 2, 16:32, :] * arriving + top
         for c in range(16):
             cols = slice(c * 128, c * 128 + 128)
@@ -414,21 +428,21 @@
                 modal[slice(128 + s * 16, 144 + s * 16), cols] = lower
 
     def grid_block(p, o):
-        rows = pl.ds(place(lax.rem(b + o, 8)), 256)
+        rows = pl.ds(place(lon_id(o)), 256)
         send2[p, o] = product(modal[...], vh[rows, :], vl[rows, :], NT)
 
-    def across(p):
+    def across(p, first, last):
         def block(t, carry):
             grid_block(p, 2 * t + 1)
-            back_to(p, 2 * t + 1, True).start()
-            return carry
-
-        lax.fori_loop(0, 4, block, 0)
+            back_to(p, 2 * t + 1).start()
+            return carry
+
+        lax.fori_loop(first, last, block, 0)
 
     def along(p):
         def block(t, carry):
             grid_block(p, 2 * t)
-            back_to(p, 2 * t, False).start()
+            back_to(p, 2 * t).start()
             return carry
 
         lax.fori_loop(1, 4, block, 0)
@@ -448,37 +462,36 @@
     for o in range(1, 4):
         coef_on(1, o).start()
     carries(0)
-    across(0)
+    across(0, 0, 2)
     transform(1, 1)
     solve(1)
-    for o in range(1, 8, 2):
-        back_late(o).start()
+    across(0, 2, 4)
     along(0)
     carries(1)
-    across(1)
+    across(1, 0, 4)
     along(1)
     for p in range(2):
         for o in range(1, 5):
             coef_to(p, o).wait_send()
         for o in range(1, 4):
             coef_on(p, o).wait_send()
-        data_pair(p, 0).wait_send()
+        for i in range(2):
+            data_pair(p, i, 0).wait_send()
+            for o in range(1, 8):
+                data_pair(p, i, o).wait_send()
+                data_to(p, i, o).wait_send()
         for o in range(1, 8):
-            data_pair(p, o).wait_send()
             to_lon(p, o).wait_send()
-            data_to(p, o).wait_send()
-            back_to(p, o, o % 2).wait_send()
+            back_to(p, o).wait_send()
         coef_pair(p).wait_send()
         own(p).wait()
     for o in range(1, 8):
         fix_to(o).wait_send()
     for o in range(1, 8, 2):
         to_lon_late(o).wait_send()
-        back_late(o).wait_send()
-        back_late(o).wait_recv()
     for p in range(2):
         for o in range(1, 8):
-            back_to(p, o, o % 2).wait_recv()
+            back_to(p, o).wait_recv()
 
 
 def per_device(forcing, metric_lon, metric_lat, lon_weights, eigen_basis, lower_mult, pivot_inverse, upper_coef):
@@ -493,11 +506,11 @@
         vmem(band, F32), vmem(band, F32), vmem(band, F32), vmem(band, F32), vmem(band, F32), vmem(band, F32),
         vmem((256, 2048), BF16), vmem((256, 2048), BF16), vmem(band, F32),
         vmem((2, 16, 8, 128), F32), vmem((2, 16, 8, 128), F32), vmem((2, 16, 8, 128), F32),
-        vmem((2, 2, 8, 48, 128), F32), vmem((2, 2, 8, 32, 128), F32), vmem((2, 8, 128, 256), F32),
+        vmem((2, 2, 8, 48, 128), F32), vmem((2, 2, 2, 8, 16, 128), F32), vmem((2, 8, 128, 256), F32),
         vmem((8, 8, 128), F32), vmem((8, 8, 128), F32), vmem((128, 128), F32),
         dma((4,)), dma((4,)), dma((3, 16)), dma((2,)), dma((4,)), dma((4,)), dma((2, 8)), dma((2, 8)),
-        dma((2, 8)), dma((2, 8)), dma((2, 8)), dma((2, 8)), dma((2, 8)), dma((2, 8)),
-        dma((8,)), dma((8,)), dma((2, 8)), dma((2, 8)), dma((2, 8)), dma((2, 8)),
+        dma((2, 8)), dma((2, 8)), dma((2, 2, 8)), dma((2, 2, 8)), dma((2, 8)), dma((2, 8)),
+        dma((8,)), dma((8,)), dma((8,)), dma((8,)), dma((2, 2, 8)), dma((2, 2, 8)),
     ]
     return pl.pallas_call(
         kernel,

time: 73 us -> 71.6 us (0.981)
  Pallas kernels: 71.5 us -> 70.1 us
    pallas_call x1, Pallas kernels: 71.5 us -> 70.1 us  [per_device(): pl.pallas_call(kernel, out_shape=pltpu.VMEM((16, 128, 256), F32), in_spec...]
where the time goes in v4:
time: 71.6 us; the launch traced here: 71.5 us
  Pallas kernels  70.1 us (98%)
  local copies, waits for them, and re-layouts  1.32 us (2%)
    pallas_call x1, Pallas kernels, per_device(): pl.pallas_call(kernel, out_shape=pltpu.VMEM((16, 128, 256), F32), in_spec...  70.1 us

profile of v4, /device:TPU:1, one launch (start us, length us, event | category | flops | bytes accessed | tf_op | source)
XLA Modules:
  0.0 71.5 jit_solution(18048842229846780676)
XLA Ops:
  0.0 70.1 %shard_map.82 = f32[16,128,256]{2,1,0:T(8,128)S(1)} custom-call(f32[16,128,256]{2,1,0:T(8,128)} %forcing_h.1, f32[128,256]{1,0:T(8,128)} %mlon_h.1, f32[128,256]{1,0:T(8,128)} %mlat_h.1, f32[1,256]{1,0:T(1,128)} %bitcast.1, f32[2048,2048]{1,0:T(8,128)} %basis_h.1, f32[2,128,2048]{2,1,0:T(8,128)} %low_h.1, f32[2,128,2048]{2,1,0:T(8,128)} %pinv_h.1, ...), custom_call_target="tpu_custom_call" | custom-call | tf_op jit(solution)/shard_map/pallas_call | solution.py:515
  70.1 1.3 %copy.10 = f32[16,128,256]{2,1,0:T(8,128)} copy(f32[16,128,256]{2,1,0:T(8,128)S(1)} %shard_map.82) | data formatting | bytes 4194304

commit v5 on v4

--- a/solution.py
+++ b/solution.py
@@ -13,7 +13,7 @@
 NT = (((1,), (1,)), ((), ()))
 TILES = 4
 STEPS = 16
-ORDER = (1, 3, 2, 4, 6, 5, 7)
+ORDER = (1, 2, 4, 6, 3, 5, 7)
 FIRST = 96
 
 
@@ -117,17 +117,9 @@
         basis_rows(slot, slot).start()
     lane = lax.broadcasted_iota(jnp.int32, (128, 128), 1)
     lane2 = lax.broadcasted_iota(jnp.int32, (32, 256), 1)
-    columns = jnp.where(lane == 32, mlon[:, 0:1] * wlon[:, 0:1], 0.0)
-    columns = jnp.where(lane == 33, mlon[:, 255:256] * wlon[:, 255:256], columns)
-    nothing = jnp.zeros((1, 256), F32)
     for k in range(16):
-        row_first[k : k + 1, :] = fpad[k, 8:9, :]
-        row_last[k : k + 1, :] = fpad[k, 135:136, :]
-        columns = jnp.where(lane == k, fpad[k, 8:136, 255:256], columns)
-        columns = jnp.where(lane == 16 + k, fpad[k, 8:136, 0:1], columns)
-        fpad[k, 7:8, :] = nothing
-        fpad[k, 136:137, :] = nothing
-    edge[...] = columns.T[:40]
+        fpad[k, 7:8, :] = jnp.zeros((1, 256), F32)
+        fpad[k, 136:137, :] = jnp.zeros((1, 256), F32)
 
     def source(k, store, edges):
         if edges:
@@ -166,6 +158,29 @@
             src_ref=src, dst_ref=dst, send_sem=send, recv_sem=recv, device_id=peer, device_id_type=MESH
         )
 
+
+    def to_lon(p, o):
+        rows = pl.ds(0, FIRST) if p == 1 and o % 2 else pl.ds(0, 128)
+        return remote(
+            send1.at[p, o, rows], got1.at[p, b, rows], s1.at[p, o], r1.at[p, o], lon_peer(o)
+        )
+
+    def to_lon_late(o):
+        rows = pl.ds(FIRST, 128 - FIRST)
+        return remote(
+            send1.at[1, o, rows], got1.at[1, b, rows], late_s.at[o], late_r.at[o], lon_peer(o)
+        )
+
+    for o in ORDER[:4]:
+        to_lon(0, o).start()
+    columns = jnp.where(lane == 32, mlon[:, 0:1] * wlon[:, 0:1], 0.0)
+    columns = jnp.where(lane == 33, mlon[:, 255:256] * wlon[:, 255:256], columns)
+    for k in range(16):
+        row_first[k : k + 1, :] = fpad[k, 8:9, :]
+        row_last[k : k + 1, :] = fpad[k, 135:136, :]
+        columns = jnp.where(lane == k, fpad[k, 8:136, 255:256], columns)
+        columns = jnp.where(lane == 16 + k, fpad[k, 8:136, 0:1], columns)
+    edge[...] = columns.T[:40]
     halos = [
         remote(edge.at[pl.ds(0, 16)], halo_w, h_s.at[0], h_r.at[0], {"lon": lax.rem(b + 1, 8)}),
         remote(edge.at[pl.ds(16, 16)], halo_e, h_s.at[1], h_r.at[1], {"lon": lax.rem(b + 7, 8)}),
@@ -174,21 +189,7 @@
     ]
     for c in halos:
         c.start()
-
-    def to_lon(p, o):
-        rows = pl.ds(0, FIRST) if p == 1 and o % 2 else pl.ds(0, 128)
-        return remote(
-            send1.at[p, o, rows], got1.at[p, b, rows], s1.at[p, o], r1.at[p, o], lon_peer(o)
-        )
-
-    def to_lon_late(o):
-        rows = pl.ds(FIRST, 128 - FIRST)
-        return remote(
-            send1.at[1, o, rows], got1.at[1, b, rows], late_s.at[o], late_r.at[o], lon_peer(o)
-        )
-
-    for o in ORDER[:5]:
-        to_lon(0, o).start()
+    to_lon(0, ORDER[4]).start()
 
     def basis_step(t, carry):
         for slot in range(4):
@@ -462,10 +463,10 @@
     for o in range(1, 4):
         coef_on(1, o).start()
     carries(0)
-    across(0, 0, 2)
+    across(0, 0, 1)
     transform(1, 1)
     solve(1)
-    across(0, 2, 4)
+    across(0, 1, 4)
     along(0)
     carries(1)
     across(1, 0, 4)

time: 71.6 us -> 71.3 us (level)
  no operation moved by 1% of the time
where the time goes in v5:
time: 71.3 us; the launch traced here: 71.2 us
  Pallas kernels  69.8 us (98%)
  local copies, waits for them, and re-layouts  1.32 us (2%)
    pallas_call x1, Pallas kernels, per_device(): pl.pallas_call(kernel, out_shape=pltpu.VMEM((16, 128, 256), F32), in_spec...  69.8 us

profile of v5, /device:TPU:1, one launch (start us, length us, event | category | flops | bytes accessed | tf_op | source)
XLA Modules:
  0.0 71.2 jit_solution(9084026450138990065)
XLA Ops:
  0.0 69.8 %shard_map.82 = f32[16,128,256]{2,1,0:T(8,128)S(1)} custom-call(f32[16,128,256]{2,1,0:T(8,128)} %forcing_h.1, f32[128,256]{1,0:T(8,128)} %mlon_h.1, f32[128,256]{1,0:T(8,128)} %mlat_h.1, f32[1,256]{1,0:T(1,128)} %bitcast.1, f32[2048,2048]{1,0:T(8,128)} %basis_h.1, f32[2,128,2048]{2,1,0:T(8,128)} %low_h.1, f32[2,128,2048]{2,1,0:T(8,128)} %pinv_h.1, ...), custom_call_target="tpu_custom_call" | custom-call | tf_op jit(solution)/shard_map/pallas_call | solution.py:516
  69.9 1.3 %copy.10 = f32[16,128,256]{2,1,0:T(8,128)} copy(f32[16,128,256]{2,1,0:T(8,128)S(1)} %shard_map.82) | data formatting | bytes 4194304
